TPU v7x, 32 devices: a whole 2x2x4 slice. The times are simulated.
32 devices in a mesh: dp: 16 (over z, y, core), mp: 2 (over x).
Axes of the slice: x: 2, y: 2, z: 4, core: 2. Of those that a mesh axis runs over, the one named last changes fastest.
Arguments:
- inputs: bfloat16 [8192, 2048], P('dp', 'mp'), may hold values from -6 to 6
- grad_moved: bfloat16 [8192, 2048], P('dp', 'mp'), may hold values from -6 to 6
- moved: int32 [16, 4], P('dp'), may hold values from 0 to 1, as said below
- segments: int32 [8192], P('dp'), may hold values from 0 to 511, as said below
- input_norm_gain: float32 [2048], replicated, may hold values from 0.5 to 1.5
- proj_in: bfloat16 [2048, 3072], P(None, 'mp'), may hold values from -0.125 to 0.125
- proj_out: bfloat16 [1024, 2048], P('mp'), may hold values from -0.1875 to 0.1875
Outputs:
- input_gradient: bfloat16 [8192, 2048], P('dp', 'mp')
- grad_proj_in: float32 [2048, 3072], P('dp', 'mp')
- grad_proj_out: float32 [1024, 2048], P('mp', 'dp')
Inputs may be any that keep to these rules, and one draw needn't show every extreme that they name: moved[g] equals moved[g XOR (8)] for every group g: blocks are swapped between partner groups slot for slot. `segments`: within each group of 512 rows the history numbers start at 0 on its first row, never fall and rise by at most one from row to row; histories never cross groups; in some group every event is a history of its own.
All inputs are finite; a program needn't handle non-finite values.
Results may differ from a plain program's by a relative error of at most 0.011.
Values may be sent and summed in bfloat16 or wider, within the bound.
A program may use at most 128 MiB of HBM per device.

v0:
```python
import jax
import jax.numpy as jnp
from jax import lax
from jax.sharding import PartitionSpec as P

DV = 128
DQK = 64
BLOCK = 128


epsilon = 1e-05
head_floor = 1.0


def swapped(block, axis, apart):
    count = lax.axis_size(axis)
    route = []
    for low in range(count):
        high = low | 1 << apart
        if high != low and high < count:
            route += [(low, high), (high, low)]
    return lax.ppermute(block, axis, route)


def forward_heads(acts, visible, heads_here):
    span = 2 * DV + 2 * DQK
    rows = acts.shape[0]
    parts = acts.reshape(rows, heads_here, span)
    u_vals = parts[:, :, :DV]
    v_vals = parts[:, :, DV : 2 * DV]
    q_vals = parts[:, :, 2 * DV : 2 * DV + DQK]
    k_vals = parts[:, :, 2 * DV + DQK :]
    scores = jnp.einsum("qhd,khd->hqk", q_vals, k_vals, preferred_element_type=jnp.float32)
    sig_s = jax.nn.sigmoid(scores)
    attend = (scores * sig_s * visible[None]).astype(jnp.bfloat16)
    slope = sig_s * (1.0 + scores * (1.0 - sig_s))
    outvals = jnp.einsum("hqk,khd->qhd", attend, v_vals, preferred_element_type=jnp.float32)
    mean_shifted = outvals - jnp.mean(outvals, axis=-1, keepdims=True)
    head_inv = lax.rsqrt(jnp.mean(mean_shifted * mean_shifted, axis=-1, keepdims=True) + head_floor)
    onorm = mean_shifted * head_inv
    mixed = (onorm * u_vals).astype(jnp.bfloat16).reshape(rows, heads_here * DV)
    saved = (u_vals, v_vals, q_vals, k_vals, attend, slope, onorm, head_inv)
    return (mixed, saved)


def backward_heads(saved, grad_mix, visible, heads_here):
    u_vals, v_vals, q_vals, k_vals, attend, slope, onorm, head_inv = saved
    rows = grad_mix.shape[0]
    grad_mixr = grad_mix.reshape(rows, heads_here, DV)
    grad_u = grad_mixr * onorm
    gon = grad_mixr * u_vals
    grad_o = (
        head_inv
        * (
            gon
            - jnp.mean(gon, axis=-1, keepdims=True)
            - onorm * jnp.mean(gon * onorm, axis=-1, keepdims=True)
        )
    ).astype(jnp.bfloat16)
    grad_att = jnp.einsum("qhd,khd->hqk", grad_o, v_vals, preferred_element_type=jnp.float32)
    grad_v = jnp.einsum("hqk,qhd->khd", attend, grad_o, preferred_element_type=jnp.float32)
    grad_scores = (grad_att * visible[None] * slope).astype(jnp.bfloat16)
    grad_q = jnp.einsum("hqk,khd->qhd", grad_scores, k_vals, preferred_element_type=jnp.float32)
    grad_k = jnp.einsum("hqk,qhd->khd", grad_scores, q_vals, preferred_element_type=jnp.float32)
    grad_act = jnp.concatenate([grad_u, grad_v, grad_q, grad_k], axis=-1)
    return grad_act.reshape(rows, heads_here * (2 * DV + 2 * DQK))


def on_device(inputs, grad_moved, moved, segments, input_norm_gain, proj_in, proj_out):
    rows = inputs.shape[0]
    span = 2 * DV + 2 * DQK
    heads_here = proj_in.shape[1] // span
    top_bit = lax.axis_size("dp").bit_length() - 2
    partner = swapped(grad_moved, "dp", top_bit)
    blocks = rows // BLOCK
    flags = moved[0][:, None, None] == 1
    returned = jnp.where(
        flags, partner.reshape(blocks, BLOCK, -1), grad_moved.reshape(blocks, BLOCK, -1)
    ).reshape(rows, -1)
    full_x, full_dy = (
        lax.all_gather(inputs, "mp", axis=1, tiled=True),
        lax.all_gather(returned, "mp", axis=1, tiled=True),
    )
    xfull = full_x.astype(jnp.float32)
    mean_shifted = xfull - jnp.mean(xfull, axis=1, keepdims=True)
    inverse_deviation = lax.rsqrt(
        jnp.mean(mean_shifted * mean_shifted, axis=1, keepdims=True) + epsilon
    )
    standardized_input = mean_shifted * inverse_deviation
    normalized_rows = (standardized_input * input_norm_gain[None, :]).astype(jnp.bfloat16)
    pre = jnp.dot(normalized_rows, proj_in, preferred_element_type=jnp.float32)
    sig_p = jax.nn.sigmoid(pre)
    acts = (pre * sig_p).astype(jnp.bfloat16)
    grad_mix = lax.dot_general(
        full_dy, proj_out, (((1,), (1,)), ((), ())), preferred_element_type=jnp.float32
    )
    order = jnp.arange(rows, dtype=jnp.int32)
    visible = (
        (segments[:, None] == segments[None, :]) & (order[None, :] <= order[:, None])
    ).astype(jnp.float32)
    mixed, saved = forward_heads(acts, visible, heads_here)
    grad_act = backward_heads(saved, grad_mix, visible, heads_here)
    partial_out = lax.dot_general(
        mixed, full_dy, (((0,), (0,)), ((), ())), preferred_element_type=jnp.float32
    )
    grad_proj_out = lax.psum_scatter(partial_out, "dp", scatter_dimension=1, tiled=True)
    grad_pre = (grad_act * sig_p * (1.0 + pre * (1.0 - sig_p))).astype(jnp.bfloat16)
    partial_in = lax.dot_general(
        normalized_rows, grad_pre, (((0,), (0,)), ((), ())), preferred_element_type=jnp.float32
    )
    grad_proj_in = lax.psum_scatter(partial_in, "dp", scatter_dimension=0, tiled=True)
    normed_term = lax.dot_general(
        grad_pre, proj_in, (((1,), (1,)), ((), ())), preferred_element_type=jnp.float32
    )
    local = inputs.shape[1]
    offset = lax.axis_index("mp") * local
    grad_normed = lax.psum(normed_term.astype(jnp.bfloat16), "mp").astype(jnp.float32)
    gain_scaled = grad_normed * input_norm_gain[None, :]
    grad_full = full_dy.astype(jnp.float32) + inverse_deviation * (
        gain_scaled
        - jnp.mean(gain_scaled, axis=1, keepdims=True)
        - standardized_input * jnp.mean(gain_scaled * standardized_input, axis=1, keepdims=True)
    )
    input_gradient = lax.dynamic_slice_in_dim(grad_full, offset, local, 1).astype(jnp.bfloat16)
    return (input_gradient, grad_proj_in, grad_proj_out)


def solution(mesh):
    return jax.shard_map(
        on_device,
        mesh=mesh,
        in_specs=(
            P("dp", "mp"),
            P("dp", "mp"),
            P("dp", None),
            P("dp"),
            P(),
            P(None, "mp"),
            P("mp", None),
        ),
        out_specs=(P("dp", "mp"), P("dp", "mp"), P("mp", "dp")),
        check_vma=False,
    )
```

profile of v0, /device:TPU:0, one launch (start us, length us, event | category | flops | bytes accessed | tf_op | source)
XLA Modules:
  0.0 408.2 jit_solution(3940126649149491493)
XLA Ops:
  8.0 4.1 %collective-permute-start = (bf16[512,1024]{1,0:T(8,128)(2,1)}, bf16[512,1024]{1,0:T(8,128)(2,1)S(1)}, u32[]{:S(2)}, u32[]{:S(2)}) collective-permute-start(bf16[512,1024]{1,0:T(8,128)(2,1)} %param.8), channel_id=1, source_target_pairs={{0,16},{16,0},{2,18},{18,2},{4,20},{20,4},{6,22},{22,6},{8,24},{24... | collective-permute-start | bytes 3145736 | tf_op jit(solution)/shard_map/ppermute | solution.py:22
  13.8 44.2 %collective-permute-done = bf16[512,1024]{1,0:T(8,128)(2,1)S(1)} collective-permute-done((bf16[512,1024]{1,0:T(8,128)(2,1)}, bf16[512,1024]{1,0:T(8,128)(2,1)S(1)}, u32[]{:S(2)}, u32[]{:S(2)}) %collective-permute-start) | collective-permute-done | bytes 1048608 | tf_op jit(solution)/shard_map/ppermute | solution.py:22
  57.9 2.4 broadcast_select_fusion
  60.5 2.1 convert_reduce_fusion
  63.4 8.2 %multiply_convert_fusion.4 = (bf16[512,1536]{1,0:T(8,128)(2,1)}, f32[512,1536]{1,0:T(8,128)}) fusion(bf16[2048,1536]{1,0:T(8,128)(2,1)} %param.12, f32[2048]{0:T(1024)S(1)} %copy-done.13, f32[512]{0:T(512)S(1)} %add_rsqrt_fusion.1, f32[512]{0:T(512)S(1)} %broadcast_multiply_fusion.5, bf16[512,2048]{1,0:T(8,128)(2,1)S(1)} %copy-done.2), kind=kOutput, calls=%fused_computation.13 | convolution fusion | flops 3230400512 | bytes 13119488 | tf_op jit(solution)/shard_map/dot_general | solution.py:91
  71.5 2.6 copy.20
  74.1 4.3 %multiply_convert_fusion.1 = (bf16[4,512,512]{2,1,0:T(8,128)(2,1)S(1)}, f32[4,512,512]{2,1,0:T(8,128)}) fusion(f32[512,512]{1,0:T(8,128)S(1)} %fusion.10, bf16[512,4,384]{0,2,1:T(8,128)(2,1)} %bitcast.35), kind=kOutput, calls=%fused_computation.8 | convolution fusion | flops 140509184 | bytes 7864320 | tf_op jit(solution)/shard_map/qhd,khd->hqk/dot_general | solution.py:33
  78.4 1.4 copy-done.5
  79.8 1.9 fusion.24
  81.8 13.0 %all-gather.3.cloned.1.call-done = bf16[512,2048]{1,0:T(8,128)(2,1)} async-done(((bf16[512,1024]{1,0:T(8,128)(2,1)}), bf16[512,2048]{1,0:T(8,128)(2,1)}) %all-gather.3.cloned.1.call-update) | async-done | bytes 2097168 | tf_op jit(solution)/shard_map/all_gather | solution.py:82
  94.8 3.0 fusion.25
  100.5 2.1 multiply_convert_fusion
  104.6 2.0 pad_maximum_fusion
  106.6 3.5 copy.19
  110.1 3.9 multiply_convert_fusion.3
  115.2 7.7 %convolution_convert_fusion = bf16[512,2048]{1,0:T(8,128)(2,1)} fusion(bf16[512,1536]{1,0:T(8,128)(2,1)S(1)} %multiply_convert_fusion.3, bf16[2048,1536]{1,0:T(8,128)(2,1)} %param.12), kind=kOutput, calls=%fused_computation.15 | convolution fusion | flops 3222274048 | bytes 9961472 | tf_op jit(solution)/shard_map/dot_general | solution.py:112
  123.2 3.2 fusion.26
  126.5 1.5 copy-done.3
  128.0 8.4 %fusion.11 = f32[2048,1536]{1,0:T(8,128)} fusion(bf16[512,1536]{1,0:T(8,128)(2,1)} %copy-done.10, f32[2048]{0:T(1024)S(1)} %copy-done.13, bf16[512,2048]{1,0:T(8,128)(2,1)S(1)} %copy-done.3, f32[512]{0:T(512)S(1)} %add_rsqrt_fusion.1, f32[512]{0:T(512)S(1)} %broadcast_multiply_fusion.5), kind=kOutput, calls=%fused_computation.38 | convolution fusion | flops 3226468352 | bytes 16265216 | tf_op jit(solution)/shard_map/dot_general | solution.py:108
  136.4 49.7 %all-reduce.2.cloned.1.call-done = bf16[512,2048]{1,0:T(8,128)(2,1)} async-done(((bf16[512,2048]{1,0:T(8,128)(2,1)}), bf16[512,2048]{1,0:T(8,128)(2,1)}) %all-reduce.2.cloned.1.call-update) | async-done | bytes 2097168 | tf_op jit(solution)/shard_map/psum | solution.py:117
  186.1 3.0 fusion.7
  189.2 1.5 fusion.6
  190.7 72.5 %reduce-scatter.5.cloned.1.call-done = f32[512,128]{1,0:T(8,128)} async-done(((f32[512,2048]{1,0:T(8,128)}), f32[512,128]{1,0:T(8,128)}) %reduce-scatter.5.cloned.1.call-update) | async-done | bytes 262160 | tf_op jit(solution)/shard_map/reduce_scatter | solution.py:106
  263.1 138.5 %reduce-scatter.3.cloned.1.call-done = f32[128,1536]{1,0:T(8,128)} async-done(((f32[2048,1536]{1,0:T(8,128)}), f32[128,1536]{1,0:T(8,128)}) %reduce-scatter.3.cloned.1.call-update) | async-done | bytes 786448 | tf_op jit(solution)/shard_map/reduce_scatter | solution.py:111
  (56 shorter events, 9.7 us)
Async XLA Ops:
  7.2 87.6 %copy-start = (bf16[512,2048]{1,0:T(8,128)(2,1)S(1)}, bf16[512,2048]{1,0:T(8,128)(2,1)}, u32[]{:S(2)}) copy-start(bf16[512,2048]{1,0:T(8,128)(2,1)} %param.13) | copy-start | bytes 6291460
  7.2 53.3 %all-gather.5.cloned.1.call-start = ((), (), s32[]{:S(2)}) async-start(), calls=%async_computation.3 | async-start | bytes 3145728 | tf_op jit(solution)/shard_map/all_gather | solution.py:81
  7.9 86.9 %all-gather.3.cloned.1.call-start = ((), (), s32[]{:S(2)}) async-start(), calls=%async_computation.2 | async-start | bytes 3145728 | tf_op jit(solution)/shard_map/all_gather | solution.py:82
  8.0 50.0 %collective-permute-start = (bf16[512,1024]{1,0:T(8,128)(2,1)}, bf16[512,1024]{1,0:T(8,128)(2,1)S(1)}, u32[]{:S(2)}, u32[]{:S(2)}) collective-permute-start(bf16[512,1024]{1,0:T(8,128)(2,1)} %param.8), channel_id=1, source_target_pairs={{0,16},{16,0},{2,18},{18,2},{4,20},{20,4},{6,22},{22,6},{8,24},{24... | collective-permute-start | bytes 3145736 | tf_op jit(solution)/shard_map/ppermute | solution.py:22
  13.8 60.4 %copy-start.11 = (f32[512,512]{1,0:T(8,128)}, f32[512,512]{1,0:T(8,128)S(1)}, u32[]{:S(2)}) copy-start(f32[512,512]{1,0:T(8,128)S(1)} %fusion.10) | copy-start | bytes 3145732
  60.3 3.0 copy-start.13
  60.4 125.7 %all-reduce.2.cloned.1.call-start = ((), (), s32[]{:S(2)}) async-start(), calls=%async_computation.4 | async-start | bytes 4194304 | tf_op jit(solution)/shard_map/psum | solution.py:117
  60.4 2.2 copy-start.2
  78.4 1.4 copy-start.5
  94.8 3.0 copy-start.4
  97.8 1.6 copy-start.12
  97.8 2.7 copy-start.14
  102.6 1.6 copy-start.6
  114.1 1.1 copy-start.10
  115.2 8.0 %copy-start.7 = (bf16[512,2048]{1,0:T(8,128)(2,1)S(1)}, bf16[512,2048]{1,0:T(8,128)(2,1)}, u32[]{:S(2)}) copy-start(bf16[512,2048]{1,0:T(8,128)(2,1)} %all-gather.3.cloned.1.call-done) | copy-start | bytes 6291460
  115.2 8.0 %copy-start.9 = (bf16[512,4,128]{0,2,1:T(8,128)(2,1)S(1)}, bf16[512,4,128]{0,2,1:T(8,128)(2,1)}, u32[]{:S(2)}) copy-start(bf16[512,4,128]{0,2,1:T(8,128)(2,1)} %get-tuple-element.7) | copy-start | bytes 1572868
  122.9 140.2 %reduce-scatter.5.cloned.1.call-start = ((), (), s32[]{:S(2)}) async-start(), calls=%async_computation.6 | async-start | bytes 4456448 | tf_op jit(solution)/shard_map/reduce_scatter | solution.py:106
  126.4 1.6 copy-start.3
  126.4 275.3 %reduce-scatter.3.cloned.1.call-start = ((), (), s32[]{:S(2)}) async-start(), calls=%async_computation.5 | async-start | bytes 13369344 | tf_op jit(solution)/shard_map/reduce_scatter | solution.py:111
  186.1 3.1 copy-start.8
  189.1 212.5 %copy-start.1 = (bf16[512,2048]{1,0:T(8,128)(2,1)S(1)}, bf16[512,2048]{1,0:T(8,128)(2,1)}, u32[]{:S(2)}) copy-start(bf16[512,2048]{1,0:T(8,128)(2,1)} %param.13) | copy-start | bytes 6291460
Sparse Core Ops, SparseCore 0:
  9.5 35.8 all-gather.4
  60.5 34.2 all-gather.2
  123.1 62.9 all-reduce.1
  190.4 72.7 reduce-scatter.4
  267.6 134.0 reduce-scatter.2
where the time goes:
time: 409 us; the launch traced here: 408 us
  waiting for transfers between devices  319 us (78%)
  matrix products  40.3 us (10%)
  other arithmetic  19 us (5%)
  between operations  14 us (3%)
  local copies, waits for them, and re-layouts  11.9 us (3%)
  starting transfers between devices  4.51 us (1%)
    reduce_scatter x1, waiting for transfers between devices, on_device(): lax.psum_scatter(partial_in, 'dp', scatter_dimension=0, tiled=True)  139 us
    reduce_scatter x1, waiting for transfers between devices, on_device(): lax.psum_scatter(partial_out, 'dp', scatter_dimension=1, tiled=True)  72.5 us
    psum x1, waiting for transfers between devices, on_device(): lax.psum(normed_term.astype(jnp.bfloat16), 'mp').astype(jnp.float32)  49.7 us
    ppermute x1, waiting for transfers between devices, swapped(): return lax.ppermute(block, axis, route)  44.2 us
    all_gather x1, waiting for transfers between devices, on_device(): lax.all_gather(returned, 'mp', axis=1, tiled=True)  13 us
    dot_general x1, matrix products, on_device(): lax.dot_general(normalized_rows, grad_pre, (((0,), (0,)), ((), ())), pref...  8.41 us
  transfers between devices with their start and end apart: 6, of which 5 were waited for; matrix products, arithmetic and copies ran while one was open for 10% of the time, Pallas kernels for 0%

commit v1 on v0

--- a/solution.py
+++ b/solution.py
@@ -1,6 +1,8 @@
 import jax
 import jax.numpy as jnp
 from jax import lax
+from jax.experimental import pallas as pl
+from jax.experimental.pallas import tpu as pltpu
 from jax.sharding import PartitionSpec as P
 
 DV = 128
@@ -20,6 +22,16 @@
         if high != low and high < count:
             route += [(low, high), (high, low)]
     return lax.ppermute(block, axis, route)
+
+
+def gathered(block):
+    if lax.axis_size("mp") != 2:
+        return lax.all_gather(block, "mp", axis=1, tiled=True)
+    other = lax.ppermute(block, "mp", [(0, 1), (1, 0)])
+    first = lax.axis_index("mp") == 0
+    return jnp.concatenate(
+        [jnp.where(first, block, other), jnp.where(first, other, block)], axis=1
+    )
 
 
 def forward_heads(acts, visible, heads_here):
@@ -66,21 +78,256 @@
     return grad_act.reshape(rows, heads_here * (2 * DV + 2 * DQK))
 
 
+MESH = pl.DeviceIdType.MESH
+
+
+def reduce_kernel(
+    normed_ref, pre_ref, dy_ref, mixed_ref, term_ref, sums_ref,
+    gin_ref, gout_ref, rterm_ref, rsums_ref,
+    own, send_c, recv_c, send_y, recv_y, keep_y, send_z, from_low, from_high, land_t, land_s,
+    sem_cs, sem_cr, sem_ys, sem_yr, sem_zs, sem_low, sem_high, sem_xs, sem_xr,
+):
+    wide = pre_ref.shape[1]
+    d = lax.axis_index("dp")
+    x = lax.axis_index("mp")
+    z = d // 4
+    y = (d // 2) % 2
+    c = d % 2
+    upper = z // 2
+    inner = (z + upper) % 2
+    core_peer = d + 1 - 2 * c
+    y_peer = d + 2 - 4 * y
+
+    barrier = pltpu.get_barrier_semaphore()
+
+    def greet(where):
+        pl.semaphore_signal(barrier, inc=1, device_id=where, device_id_type=MESH)
+
+    greet({"dp": core_peer})
+    greet({"dp": y_peer})
+    greet({"mp": 1 - x})
+
+    @pl.when(z > 0)
+    def _():
+        greet({"dp": d - 4})
+
+    @pl.when(z < 3)
+    def _():
+        greet({"dp": d + 4})
+
+    pl.semaphore_wait(barrier, 3 + (z + 3) // 4 + (6 - z) // 4)
+
+    def remote(src, dst, send_sem, recv_sem, where):
+        return pltpu.make_async_remote_copy(
+            src_ref=src, dst_ref=dst, send_sem=send_sem, recv_sem=recv_sem,
+            device_id=where, device_id_type=MESH,
+        )
+
+    cross_t = remote(term_ref, land_t, sem_xs.at[0], sem_xr.at[0], {"mp": 1 - x})
+    cross_s = remote(sums_ref, land_s, sem_xs.at[1], sem_xr.at[1], {"mp": 1 - x})
+    cross_t.start()
+    cross_s.start()
+
+    def target(k):
+        v = (3 - k) + (k // 2) * inner * (2 * k - 5)
+        return (1 - upper) * v + upper * (3 - v)
+
+    def product(slot, core):
+        k = slot % 4
+        side = (1 - slot // 4) * (1 - y) + (slot // 4) * y
+        chunk = target(k) * 4 + side * 2 + core
+        cols = pl.ds(pl.multiple_of(chunk * 128, 128), 128)
+        left = lax.dot_general(
+            normed_ref[:, cols], pre_ref[...], (((0,), (0,)), ((), ())),
+            preferred_element_type=jnp.float32,
+        )
+        right = lax.dot_general(
+            dy_ref[:, cols], mixed_ref[...], (((0,), (0,)), ((), ())),
+            preferred_element_type=jnp.float32,
+        )
+        return left, right
+
+    def to_core(slot):
+        return remote(
+            send_c.at[slot], recv_c.at[slot], sem_cs.at[slot], sem_cr.at[slot], {"dp": core_peer}
+        )
+
+    def to_y(k):
+        return remote(send_y.at[k], recv_y.at[k], sem_ys.at[k], sem_yr.at[k], {"dp": y_peer})
+
+    def issue(slot):
+        left, right = product(slot, 1 - c)
+        send_c[slot, :, :wide] = left.astype(jnp.bfloat16)
+        send_c[slot, :, wide:] = right.astype(jnp.bfloat16)
+        to_core(slot).start()
+
+    issue(0)
+
+    def step(slot, carry):
+        @pl.when(slot < 7)
+        def _():
+            issue(slot + 1)
+
+        left, right = product(slot, c)
+        own[:, :wide] = left
+        own[:, wide:] = right
+        to_core(slot).wait_recv()
+
+        @pl.when(slot < 4)
+        def _():
+            send_y[slot] = (own[...] + recv_c[slot].astype(jnp.float32)).astype(jnp.bfloat16)
+            to_y(slot).start()
+
+        @pl.when(slot >= 4)
+        def _():
+            keep_y[slot - 4] = (own[...] + recv_c[slot].astype(jnp.float32)).astype(jnp.bfloat16)
+
+        return carry
+
+    lax.fori_loop(0, 8, step, 0)
+
+    def up(k, t):
+        return remote(send_z.at[k], from_low.at[t], sem_zs.at[k], sem_low.at[t], {"dp": d + 4})
+
+    def down(k, t):
+        return remote(send_z.at[k], from_high.at[t], sem_zs.at[k], sem_high.at[t], {"dp": d - 4})
+
+    def along(k, carry):
+        t = target(k)
+        to_y(k).wait_recv()
+
+        @pl.when(t == z)
+        def _():
+            own[...] = keep_y[k].astype(jnp.float32) + recv_y[k].astype(jnp.float32)
+
+        def forward(arrived, sem, present, copy):
+            @pl.when(present)
+            def _():
+                pltpu.make_async_copy(arrived.at[t], arrived.at[t], sem.at[t]).wait()
+                send_z[k] = (
+                    keep_y[k].astype(jnp.float32)
+                    + recv_y[k].astype(jnp.float32)
+                    + arrived[t].astype(jnp.float32)
+                ).astype(jnp.bfloat16)
+
+            @pl.when(jnp.logical_not(present))
+            def _():
+                send_z[k] = (
+                    keep_y[k].astype(jnp.float32) + recv_y[k].astype(jnp.float32)
+                ).astype(jnp.bfloat16)
+
+            copy.start()
+
+        @pl.when(t > z)
+        def _():
+            forward(from_low, sem_low, z > 0, up(k, t))
+
+        @pl.when(t < z)
+        def _():
+            forward(from_high, sem_high, z < 3, down(k, t))
+
+        return carry
+
+    lax.fori_loop(0, 4, along, 0)
+
+    @pl.when(z > 0)
+    def _():
+        pltpu.make_async_copy(from_low.at[z], from_low.at[z], sem_low.at[z]).wait()
+        own[...] += from_low[z].astype(jnp.float32)
+
+    @pl.when(z < 3)
+    def _():
+        pltpu.make_async_copy(from_high.at[z], from_high.at[z], sem_high.at[z]).wait()
+        own[...] += from_high[z].astype(jnp.float32)
+
+    gin_ref[...] = own[:, :wide]
+    gout_ref[...] = own[:, wide:]
+    cross_t.wait()
+    cross_s.wait()
+    rterm_ref[...] = land_t[...]
+    rsums_ref[...] = land_s[...]
+
+    def drain(slot, carry):
+        to_core(slot).wait_send()
+        return carry
+
+    lax.fori_loop(0, 8, drain, 0)
+
+    def drain_far(k, carry):
+        to_y(k).wait_send()
+        t = target(k)
+
+        @pl.when(t > z)
+        def _():
+            up(k, t).wait_send()
+
+        @pl.when(t < z)
+        def _():
+            down(k, t).wait_send()
+
+        return carry
+
+    lax.fori_loop(0, 4, drain_far, 0)
+
+
+def reduced(normed, grad_pre, full_dy, mixed, term, sums):
+    wide, narrow = grad_pre.shape[1], mixed.shape[1]
+    total = wide + narrow
+    low, full = jnp.bfloat16, jnp.float32
+    return pl.pallas_call(
+        reduce_kernel,
+        out_shape=(
+            jax.ShapeDtypeStruct((128, wide), full),
+            jax.ShapeDtypeStruct((128, narrow), full),
+            jax.ShapeDtypeStruct(term.shape, low),
+            jax.ShapeDtypeStruct(sums.shape, full),
+        ),
+        in_specs=[pl.BlockSpec(memory_space=pltpu.VMEM)] * 6,
+        out_specs=[pl.BlockSpec(memory_space=pltpu.VMEM)] * 4,
+        scratch_shapes=[
+            pltpu.VMEM((128, total), full),
+            pltpu.VMEM((8, 128, total), low),
+            pltpu.VMEM((8, 128, total), low),
+            pltpu.VMEM((4, 128, total), low),
+            pltpu.VMEM((4, 128, total), low),
+            pltpu.VMEM((4, 128, total), low),
+            pltpu.VMEM((4, 128, total), low),
+            pltpu.VMEM((4, 128, total), low),
+            pltpu.VMEM((4, 128, total), low),
+            pltpu.VMEM(term.shape, low),
+            pltpu.VMEM(sums.shape, full),
+            pltpu.SemaphoreType.DMA((8,)),
+            pltpu.SemaphoreType.DMA((8,)),
+            pltpu.SemaphoreType.DMA((4,)),
+            pltpu.SemaphoreType.DMA((4,)),
+            pltpu.SemaphoreType.DMA((4,)),
+            pltpu.SemaphoreType.DMA((4,)),
+            pltpu.SemaphoreType.DMA((4,)),
+            pltpu.SemaphoreType.DMA((2,)),
+            pltpu.SemaphoreType.DMA((2,)),
+        ],
+        compiler_params=pltpu.CompilerParams(
+            collective_id=0, has_side_effects=True, vmem_limit_bytes=60 * 1024 * 1024
+        ),
+    )(normed, grad_pre, full_dy, mixed, term, sums)
+
+
 def on_device(inputs, grad_moved, moved, segments, input_norm_gain, proj_in, proj_out):
     rows = inputs.shape[0]
     span = 2 * DV + 2 * DQK
     heads_here = proj_in.shape[1] // span
     top_bit = lax.axis_size("dp").bit_length() - 2
-    partner = swapped(grad_moved, "dp", top_bit)
     blocks = rows // BLOCK
-    flags = moved[0][:, None, None] == 1
-    returned = jnp.where(
-        flags, partner.reshape(blocks, BLOCK, -1), grad_moved.reshape(blocks, BLOCK, -1)
-    ).reshape(rows, -1)
-    full_x, full_dy = (
-        lax.all_gather(inputs, "mp", axis=1, tiled=True),
-        lax.all_gather(returned, "mp", axis=1, tiled=True),
-    )
+    mine = [grad_moved[j * BLOCK : (j + 1) * BLOCK] for j in range(blocks)]
+    theirs = [swapped(block, "dp", top_bit) for block in mine]
+    full_x = gathered(inputs)
+    after, returned = full_x, []
+    for j in range(blocks):
+        landed, after = lax.optimization_barrier((theirs[j], after))
+        full_x = after if j == 0 else full_x
+        after = jnp.where(moved[0, j] == 1, landed, mine[j])
+        returned.append(gathered(after))
+    full_dy = jnp.concatenate(returned, axis=0)
     xfull = full_x.astype(jnp.float32)
     mean_shifted = xfull - jnp.mean(xfull, axis=1, keepdims=True)
     inverse_deviation = lax.rsqrt(
@@ -100,28 +347,48 @@
     ).astype(jnp.float32)
     mixed, saved = forward_heads(acts, visible, heads_here)
     grad_act = backward_heads(saved, grad_mix, visible, heads_here)
-    partial_out = lax.dot_general(
-        mixed, full_dy, (((0,), (0,)), ((), ())), preferred_element_type=jnp.float32
-    )
-    grad_proj_out = lax.psum_scatter(partial_out, "dp", scatter_dimension=1, tiled=True)
     grad_pre = (grad_act * sig_p * (1.0 + pre * (1.0 - sig_p))).astype(jnp.bfloat16)
-    partial_in = lax.dot_general(
-        normalized_rows, grad_pre, (((0,), (0,)), ((), ())), preferred_element_type=jnp.float32
-    )
-    grad_proj_in = lax.psum_scatter(partial_in, "dp", scatter_dimension=0, tiled=True)
+    local = inputs.shape[1]
+    offset = lax.axis_index("mp") * local
     normed_term = lax.dot_general(
         grad_pre, proj_in, (((1,), (1,)), ((), ())), preferred_element_type=jnp.float32
+    ).astype(jnp.bfloat16)
+    term_scaled = normed_term.astype(jnp.float32) * input_norm_gain[None, :]
+    sums = jnp.stack([jnp.sum(term_scaled, axis=1), jnp.sum(term_scaled * standardized_input, axis=1)])
+    if lax.axis_size("mp") == 2 and lax.axis_size("dp") == 16:
+        sent = lax.dynamic_slice_in_dim(normed_term, local - offset, local, 1)
+        kept = lax.dynamic_slice_in_dim(normed_term, offset, local, 1)
+        grad_proj_in, grad_proj_out, other_term, other_sums = reduced(
+            normalized_rows, grad_pre, full_dy, mixed, sent, sums
+        )
+        grad_proj_out = grad_proj_out.T
+        sums = sums + other_sums
+        grad_normed = kept.astype(jnp.float32) + other_term.astype(jnp.float32)
+    else:
+        partial_out = lax.dot_general(
+            mixed, full_dy, (((0,), (0,)), ((), ())), preferred_element_type=jnp.float32
+        )
+        grad_proj_out = lax.psum_scatter(
+            partial_out.astype(jnp.bfloat16), "dp", scatter_dimension=1, tiled=True
+        ).astype(jnp.float32)
+        partial_in = lax.dot_general(
+            normalized_rows, grad_pre, (((0,), (0,)), ((), ())), preferred_element_type=jnp.float32
+        )
+        grad_proj_in = lax.psum_scatter(
+            partial_in.astype(jnp.bfloat16), "dp", scatter_dimension=0, tiled=True
+        ).astype(jnp.float32)
+        sums = lax.psum(sums, "mp")
+        grad_normed = lax.psum_scatter(
+            normed_term, "mp", scatter_dimension=1, tiled=True
+        ).astype(jnp.float32)
+    means = sums / standardized_input.shape[1]
+    here = lambda array: lax.dynamic_slice_in_dim(array, offset, local, 1)
+    grad_here = here(full_dy).astype(jnp.float32) + inverse_deviation * (
+        grad_normed * here(input_norm_gain[None, :])
+        - means[0][:, None]
+        - here(standardized_input) * means[1][:, None]
     )
-    local = inputs.shape[1]
-    offset = lax.axis_index("mp") * local
-    grad_normed = lax.psum(normed_term.astype(jnp.bfloat16), "mp").astype(jnp.float32)
-    gain_scaled = grad_normed * input_norm_gain[None, :]
-    grad_full = full_dy.astype(jnp.float32) + inverse_deviation * (
-        gain_scaled
-        - jnp.mean(gain_scaled, axis=1, keepdims=True)
-        - standardized_input * jnp.mean(gain_scaled * standardized_input, axis=1, keepdims=True)
-    )
-    input_gradient = lax.dynamic_slice_in_dim(grad_full, offset, local, 1).astype(jnp.bfloat16)
+    input_gradient = grad_here.astype(jnp.bfloat16)
     return (input_gradient, grad_proj_in, grad_proj_out)
 
 

time: 409 us -> 201 us (0.49)
  waiting for transfers between devices: 319 us -> 49.8 us
  Pallas kernels: 0 us -> 61.7 us
  matrix products: 40.3 us -> 23.1 us
  other arithmetic: 19 us -> 31.7 us
  between operations: 14 us -> 3.41 us
  starting transfers between devices: 4.51 us -> 13.7 us
  local copies, waits for them, and re-layouts: 11.9 us -> 16.7 us
    reduce_scatter x2 -> x0, waiting for transfers between devices: 211 us -> none  [the longest x1 139 us: on_device(): lax.psum_scatter(partial_in, 'dp', scatter_dimension=0, tiled=True)]
    pallas_call x0 -> x1, Pallas kernels: none -> 61.7 us  [reduced(): pl.pallas_call(reduce_kernel, out_shape=(jax.ShapeDtypeStruct((128, wide)...]
    psum x1 -> x0, waiting for transfers between devices: 49.7 us -> none  [on_device(): lax.psum(normed_term.astype(jnp.bfloat16), 'mp').astype(jnp.float32)]
    ppermute x0 -> x5, waiting for transfers between devices: none -> 19.7 us  [gathered(): other = lax.ppermute(block, 'mp', [(0, 1), (1, 0)])]
    ppermute x1 -> x4, waiting for transfers between devices: 44.2 us -> 30.1 us  [swapped(): return lax.ppermute(block, axis, route)]
    concatenate x0 -> x2, other arithmetic: none -> 13.5 us  [the longest x1 13.4 us: on_device(): full_dy = jnp.concatenate(returned, axis=0)]
    all_gather x2 -> x0, waiting for transfers between devices: 13 us -> none  [the longest x1 13 us: on_device(): lax.all_gather(returned, 'mp', axis=1, tiled=True)]
    dot_general x2 -> x0, matrix products: 11.6 us -> none  [the longest x1 8.41 us: on_device(): lax.dot_general(normalized_rows, grad_pre, (((0,), (0,)), ((), ())), pref...]
  transfers between devices with their start and end apart: 6 -> 9, of which waited for: 5 -> 5; matrix products, arithmetic and copies ran while one was open for 10% -> 5% of each run, Pallas kernels for 0% -> 0%
where the time goes in v1:
time: 201 us; the launch traced here: 200 us
  Pallas kernels  61.7 us (31%)
  waiting for transfers between devices  49.8 us (25%)
  other arithmetic  31.7 us (16%)
  matrix products  23.1 us (11%)
  local copies, waits for them, and re-layouts  16.7 us (8%)
  starting transfers between devices  13.7 us (7%)
  between operations  3.41 us (2%)
    pallas_call x1, Pallas kernels, reduced(): pl.pallas_call(reduce_kernel, out_shape=(jax.ShapeDtypeStruct((128, wide)...  61.7 us
    ppermute x4, waiting for transfers between devices, swapped(): return lax.ppermute(block, axis, route)  30.1 us
    ppermute x5, waiting for transfers between devices, gathered(): other = lax.ppermute(block, 'mp', [(0, 1), (1, 0)])  19.7 us
    concatenate x1, other arithmetic, on_device(): full_dy = jnp.concatenate(returned, axis=0)  13.4 us
    dot_general x1, matrix products, on_device(): lax.dot_general(grad_pre, proj_in, (((1,), (1,)), ((), ())), preferred_el...  8.91 us
    ppermute x5, starting transfers between devices, gathered(): other = lax.ppermute(block, 'mp', [(0, 1), (1, 0)])  8.11 us
    ppermute x4, starting transfers between devices, swapped(): return lax.ppermute(block, axis, route)  5.63 us
    dot_general x1, matrix products, on_device(): pre = jnp.dot(normalized_rows, proj_in, preferred_element_type=jnp.float32)  5.33 us
  transfers between devices with their start and end apart: 9, of which 5 were waited for; matrix products, arithmetic and copies ran while one was open for 5% of the time, Pallas kernels for 0%

profile of v1, /device:TPU:0, one launch (start us, length us, event | category | flops | bytes accessed | tf_op | source)
XLA Modules:
  0.0 200.1 jit_solution(5153552425698577532)
XLA Ops:
  0.6 3.0 %collective-permute-start.1 = (bf16[512,1024]{1,0:T(8,128)(2,1)}, bf16[512,1024]{1,0:T(8,128)(2,1)S(1)}, u32[]{:S(2)}, u32[]{:S(2)}) collective-permute-start(bf16[512,1024]{1,0:T(8,128)(2,1)} %param.7), channel_id=1, source_target_pairs={{0,1},{1,0},{2,3},{3,2},{4,5},{5,4},{6,7},{7,6},{8,9},{9,8},{10,11... | collective-permute-start | bytes 3145736 | tf_op jit(solution)/shard_map/ppermute | solution.py:30
  3.7 1.7 slice.43
  5.3 2.6 %collective-permute-start = (bf16[128,1024]{1,0:T(8,128)(2,1)}, bf16[128,1024]{1,0:T(8,128)(2,1)S(1)}, u32[]{:S(2)}, u32[]{:S(2)}) collective-permute-start(bf16[128,1024]{1,0:T(8,128)(2,1)} %slice.43), channel_id=1, source_target_pairs={{0,16},{16,0},{2,18},{18,2},{4,20},{20,4},{6,22},{22,6},{8,24},{24... | collective-permute-start | bytes 786440 | tf_op jit(solution)/shard_map/ppermute | solution.py:24
  11.8 1.9 fusion.6
  13.7 13.3 %collective-permute-done.1 = bf16[512,1024]{1,0:T(8,128)(2,1)S(1)} collective-permute-done((bf16[512,1024]{1,0:T(8,128)(2,1)}, bf16[512,1024]{1,0:T(8,128)(2,1)S(1)}, u32[]{:S(2)}, u32[]{:S(2)}) %collective-permute-start.1) | collective-permute-done | bytes 1048608 | tf_op jit(solution)/shard_map/ppermute | solution.py:30
  27.1 1.5 broadcast_select_fusion.1
  31.3 5.3 %multiply_convert_fusion.4 = (bf16[512,1536]{1,0:T(8,128)(2,1)}, f32[512,1536]{1,0:T(8,128)}) fusion(bf16[512,2048]{1,0:T(8,128)(2,1)S(1)} %multiply_convert_fusion.2.normed_ref, bf16[2048,1536]{1,0:T(8,128)(2,1)S(1)} %bitcast.54), kind=kOutput, calls=%fused_computation.14 | convolution fusion | flops 3225157632 | bytes 13107200 | tf_op jit(solution)/shard_map/dot_general | solution.py:338
  36.7 2.7 %copy.23 = bf16[512,1536]{0,1:T(8,128)(2,1)} copy(bf16[512,1536]{1,0:T(8,128)(2,1)} %get-tuple-element.53) | data formatting | bytes 3145728 | tf_op jit(solution)/shard_map/reshape | solution.py:40
  39.4 2.9 %collective-permute-start.3 = (bf16[128,1024]{1,0:T(8,128)(2,1)S(1)}, bf16[128,1024]{1,0:T(8,128)(2,1)S(1)}, u32[]{:S(2)}, u32[]{:S(2)}) collective-permute-start(bf16[128,1024]{1,0:T(8,128)(2,1)S(1)} %get-tuple-element.38), channel_id=1, source_target_pairs={{0,16},{16,0},{2,18},{18,2},{4,20},{20,4},{6,22},{22,6},{8,24},{24... | collective-permute-start | bytes 786440 | tf_op jit(solution)/shard_map/ppermute | solution.py:24
  43.8 3.0 %multiply_convert_fusion.1 = (bf16[4,512,512]{2,1,0:T(8,128)(2,1)S(1)}, f32[4,512,512]{2,1,0:T(8,128)S(1)}) fusion(f32[512,512]{1,0:T(8,128)} %fusion.6, bf16[512,4,384]{0,2,1:T(8,128)(2,1)} %bitcast.38), kind=kOutput, calls=%fused_computation.9 | convolution fusion | flops 140509184 | bytes 7864320 | tf_op jit(solution)/shard_map/qhd,khd->hqk/dot_general | solution.py:45
  47.7 5.8 %collective-permute-done.3 = bf16[128,1024]{1,0:T(8,128)(2,1)S(1)} collective-permute-done((bf16[128,1024]{1,0:T(8,128)(2,1)S(1)}, bf16[128,1024]{1,0:T(8,128)(2,1)S(1)}, u32[]{:S(2)}, u32[]{:S(2)}) %collective-permute-start.3) | collective-permute-done | bytes 262176 | tf_op jit(solution)/shard_map/ppermute | solution.py:24
  53.8 13.6 %collective-permute-done.5 = bf16[128,1024]{1,0:T(8,128)(2,1)S(1)} collective-permute-done((bf16[128,1024]{1,0:T(8,128)(2,1)S(1)}, bf16[128,1024]{1,0:T(8,128)(2,1)S(1)}, u32[]{:S(2)}, u32[]{:S(2)}) %collective-permute-start.5) | collective-permute-done | bytes 262176 | tf_op jit(solution)/shard_map/ppermute | solution.py:24
  69.7 10.7 %collective-permute-done.7 = bf16[128,1024]{1,0:T(8,128)(2,1)S(1)} collective-permute-done((bf16[128,1024]{1,0:T(8,128)(2,1)S(1)}, bf16[128,1024]{1,0:T(8,128)(2,1)S(1)}, u32[]{:S(2)}, u32[]{:S(2)}) %collective-permute-start.7) | collective-permute-done | bytes 262176 | tf_op jit(solution)/shard_map/ppermute | solution.py:24
  82.0 6.4 %collective-permute-done.8 = bf16[128,1024]{1,0:T(8,128)(2,1)S(1)} collective-permute-done((bf16[128,1024]{1,0:T(8,128)(2,1)S(1)}, bf16[128,1024]{1,0:T(8,128)(2,1)S(1)}, u32[]{:S(2)}, u32[]{:S(2)}) %collective-permute-start.8) | collective-permute-done | bytes 262176 | tf_op jit(solution)/shard_map/ppermute | solution.py:30
  88.4 13.4 %maximum_maximum_fusion.dy_ref = bf16[512,2048]{1,0:T(8,128)(2,1)S(1)} fusion(bf16[128,1024]{1,0:T(8,128)(2,1)S(1)} %get-tuple-element.46, bf16[128,1024]{1,0:T(8,128)(2,1)S(1)} %get-tuple-element.45, bf16[128,1024]{1,0:T(8,128)(2,1)S(1)} %get-tuple-element.44, bf16[128,1024]{1,0:T(8,128)(2,1)S(1)} %get-tuple-element.43, ...), kind=kLoop, calls=%fused_computation.18 | loop fusion | flops 16777216 | bytes 4194304 | tf_op jit(solution)/shard_map/concatenate | solution.py:330
  104.5 2.1 %multiply_convert_fusion = bf16[4,512,512]{2,1,0:T(8,128)(2,1)S(1)} fusion(f32[4,512,512]{2,1,0:T(8,128)S(1)} %get-tuple-element.56, bf16[512,4,128]{0,2,1:T(8,128)(2,1)S(1)} %multiply_convert_fusion.5, f32[512,512]{1,0:T(8,128)S(1)} %copy-done.9, bf16[512,4,384]{0,2,1:T(8,128)(2,1)S(1)} %bitcast.42), kind=kOutput, calls=%fused_computation.8 | convolution fusion | flops 278921216 | bytes 8388608 | tf_op jit(solution)/shard_map/qhd,khd->hqk/dot_general | solution.py:72
  108.3 2.0 %pad_maximum_fusion = f32[512,4,384]{0,2,1:T(8,128)} fusion(f32[512,4,64]{0,2,1:T(8,128)S(1)} %convolution_bitcast_fusion.2, f32[512,4,64]{0,2,1:T(8,128)S(1)} %convolution_bitcast_fusion.3, f32[512,4,128]{0,2,1:T(8,128)S(1)} %convolution_bitcast_fusion, f32[512,4,128]{0,2,1:T(8,128)S(1)} %get-tuple-element.32), kind=kLoop, calls=%fused_computation.12 | loop fusion | flops 2359296 | bytes 6291456 | tf_op jit(solution)/shard_map/concatenate | solution.py:77
  110.3 3.6 %copy.21 = f32[512,1536]{1,0:T(8,128)} copy(f32[512,1536]{0,1:T(8,128)} %bitcast.37) | data formatting | bytes 6291456 | tf_op jit(solution)/shard_map/reshape | solution.py:78
  113.9 4.1 %multiply_convert_fusion.3.pre_ref = bf16[512,1536]{1,0:T(8,128)(2,1)S(1)} fusion(f32[512,1536]{1,0:T(8,128)} %get-tuple-element.54, f32[512,1536]{1,0:T(8,128)} %copy.21), kind=kLoop, calls=%fused_computation.13 | loop fusion | flops 7077888 | bytes 7864320 | tf_op jit(solution)/shard_map/convert_element_type | solution.py:350
  118.0 8.9 %fusion.3 = (f32[512]{0:T(512)S(1)}, f32[512]{0:T(512)S(1)}, f32[512,2048]{1,0:T(8,128)}, bf16[512,2048]{1,0:T(8,128)(2,1)}) fusion(f32[2048]{0:T(1024)S(1)} %copy-done.11, f32[512]{0:T(512)S(1)} %add_rsqrt_fusion.1, f32[512]{0:T(512)S(1)} %broadcast_multiply_fusion.3, bf16[512,2048]{1,0:T(8,128)(2,1)S(1)} %copy-done.3, ...), kind=kOutput, calls=%fused_computation.7 | convolution fusion | flops 3230661632 | bytes 16269312 | tf_op jit(solution)/shard_map/dot_general | solution.py:353
  127.9 2.3 %constant_dynamic-slice_fusion.term_ref = bf16[512,1024]{1,0:T(8,128)(2,1)} fusion(bf16[512,2048]{1,0:T(8,128)(2,1)} %get-tuple-element.59, s32[]{:T(128)S(6)} %select_n.102), kind=kLoop, calls=%fused_computation.65 | loop fusion | bytes 2097156 | tf_op jit(solution)/shard_map/dynamic_slice | solution.py:359
  130.7 61.7 %shard_map.94 = (f32[128,1536]{1,0:T(8,128)}, f32[128,512]{1,0:T(8,128)}, bf16[512,1024]{1,0:T(8,128)(2,1)}, f32[2,512]{1,0:T(2,128)}) custom-call(bf16[512,2048]{1,0:T(8,128)(2,1)} %copy-done.6, bf16[512,1536]{1,0:T(8,128)(2,1)} %copy-done.7, bf16[512,2048]{1,0:T(8,128)(2,1)} %copy-done.4, bf16[512,512]{1,0:T(8,128)(2,1)} %copy.22.mixed_ref, ...), custom_call_target="tpu_custom_call" | custom-call | tf_op jit(solution)/shard_map/pallas_call | solution.py:277
  193.1 1.8 copy.18
  194.9 4.3 %add_convert_fusion = bf16[512,1024]{1,0:T(8,128)(2,1)} fusion(f32[512,2048]{1,0:T(8,128)} %get-tuple-element.29, s32[]{:T(128)} %select_n.101, bf16[512,1024]{1,0:T(8,128)(2,1)} %get-tuple-element.17, f32[512]{0:T(512)S(1)} %bitcast.48, f32[512]{0:T(512)S(1)} %bitcast.47, f32[1024]{0:T(1024)S(1)} %dynamic-slice-done, ...), kind=kLoop, calls=%fused_computation.19 | loop fusion | flops 5767168 | bytes 6301700 | tf_op jit(solution)/shard_map/convert_element_type | solution.py:391
  (72 shorter events, 18.2 us)
Async XLA Ops:
  0.6 101.2 %copy-start = (bf16[512,2048]{1,0:T(8,128)(2,1)S(1)}, bf16[512,2048]{1,0:T(8,128)(2,1)}, u32[]{:S(2)}) copy-start(bf16[512,2048]{1,0:T(8,128)(2,1)} %param.13) | copy-start | bytes 6291460
  0.6 26.4 %collective-permute-start.1 = (bf16[512,1024]{1,0:T(8,128)(2,1)}, bf16[512,1024]{1,0:T(8,128)(2,1)S(1)}, u32[]{:S(2)}, u32[]{:S(2)}) collective-permute-start(bf16[512,1024]{1,0:T(8,128)(2,1)} %param.7), channel_id=1, source_target_pairs={{0,1},{1,0},{2,3},{3,2},{4,5},{5,4},{6,7},{7,6},{8,9},{9,8},{10,11... | collective-permute-start | bytes 3145736 | tf_op jit(solution)/shard_map/ppermute | solution.py:30
  5.3 23.4 %collective-permute-start = (bf16[128,1024]{1,0:T(8,128)(2,1)}, bf16[128,1024]{1,0:T(8,128)(2,1)S(1)}, u32[]{:S(2)}, u32[]{:S(2)}) collective-permute-start(bf16[128,1024]{1,0:T(8,128)(2,1)} %slice.43), channel_id=1, source_target_pairs={{0,16},{16,0},{2,18},{18,2},{4,20},{20,4},{6,22},{22,6},{8,24},{24... | collective-permute-start | bytes 786440 | tf_op jit(solution)/shard_map/ppermute | solution.py:24
  27.1 3.5 %slice-start = ((s8[6291456]{0:T(1024)(128)(4,1)}), s8[4194304]{0:T(1024)(128)(4,1)S(1)}, s32[]{:S(2)}) async-start(s8[6291456]{0:T(1024)(128)(4,1)} %bitcast.53), calls=%async_computation.1 | async-start | bytes 8388608
  28.8 1.8 copy-start.2
  28.8 1.1 copy-start.11
  28.8 2.5 %slice-start.1 = ((s8[6291456]{0:T(1024)(128)(4,1)}), s8[2097152]{0:T(1024)(128)(4,1)S(1)}, s32[]{:S(2)}) async-start(s8[6291456]{0:T(1024)(128)(4,1)} %bitcast.53), calls=%async_computation.2 | async-start | bytes 4194304
  31.3 5.3 %copy-start.6 = (bf16[512,2048]{1,0:T(8,128)(2,1)}, bf16[512,2048]{1,0:T(8,128)(2,1)S(1)}, u32[]{:S(2)}) copy-start(bf16[512,2048]{1,0:T(8,128)(2,1)S(1)} %multiply_convert_fusion.2.normed_ref) | copy-start | bytes 6291460
  36.7 2.7 %copy-start.8 = (bf16[512,1024]{1,0:T(8,128)(2,1)S(1)}, bf16[512,1024]{1,0:T(8,128)(2,1)}, u32[]{:S(2)}) copy-start(bf16[512,1024]{1,0:T(8,128)(2,1)} %param.8) | copy-start | bytes 3145732
  39.4 14.0 %collective-permute-start.3 = (bf16[128,1024]{1,0:T(8,128)(2,1)S(1)}, bf16[128,1024]{1,0:T(8,128)(2,1)S(1)}, u32[]{:S(2)}, u32[]{:S(2)}) collective-permute-start(bf16[128,1024]{1,0:T(8,128)(2,1)S(1)} %get-tuple-element.38), channel_id=1, source_target_pairs={{0,16},{16,0},{2,18},{18,2},{4,20},{20,4},{6,22},{22,6},{8,24},{24... | collective-permute-start | bytes 786440 | tf_op jit(solution)/shard_map/ppermute | solution.py:24
  42.3 26.7 %collective-permute-start.2 = (bf16[128,1024]{1,0:T(8,128)(2,1)S(1)}, bf16[128,1024]{1,0:T(8,128)(2,1)S(1)}, u32[]{:S(2)}, u32[]{:S(2)}) collective-permute-start(bf16[128,1024]{1,0:T(8,128)(2,1)S(1)} %get-tuple-element.37), channel_id=1, source_target_pairs={{0,1},{1,0},{2,3},{3,2},{4,5},{5,4},{6,7},{7,6},{8,9},{9,8},{10,11... | collective-permute-start | bytes 786440 | tf_op jit(solution)/shard_map/ppermute | solution.py:30
  43.8 3.0 %copy-start.5 = (bf16[512,1536]{0,1:T(8,128)(2,1)S(1)}, bf16[512,1536]{0,1:T(8,128)(2,1)}, u32[]{:S(2)}) copy-start(bf16[512,1536]{0,1:T(8,128)(2,1)} %copy.23) | copy-start | bytes 4718596
  53.5 13.8 %collective-permute-start.5 = (bf16[128,1024]{1,0:T(8,128)(2,1)S(1)}, bf16[128,1024]{1,0:T(8,128)(2,1)S(1)}, u32[]{:S(2)}, u32[]{:S(2)}) collective-permute-start(bf16[128,1024]{1,0:T(8,128)(2,1)S(1)} %get-tuple-element.36), channel_id=1, source_target_pairs={{0,16},{16,0},{2,18},{18,2},{4,20},{20,4},{6,22},{22,6},{8,24},{24... | collective-permute-start | bytes 786440 | tf_op jit(solution)/shard_map/ppermute | solution.py:24
  67.4 13.0 %collective-permute-start.7 = (bf16[128,1024]{1,0:T(8,128)(2,1)S(1)}, bf16[128,1024]{1,0:T(8,128)(2,1)S(1)}, u32[]{:S(2)}, u32[]{:S(2)}) collective-permute-start(bf16[128,1024]{1,0:T(8,128)(2,1)S(1)} %get-tuple-element.34), channel_id=1, source_target_pairs={{0,16},{16,0},{2,18},{18,2},{4,20},{20,4},{6,22},{22,6},{8,24},{24... | collective-permute-start | bytes 786440 | tf_op jit(solution)/shard_map/ppermute | solution.py:24
  67.5 14.4 %collective-permute-start.4 = (bf16[128,1024]{1,0:T(8,128)(2,1)S(1)}, bf16[128,1024]{1,0:T(8,128)(2,1)S(1)}, u32[]{:S(2)}, u32[]{:S(2)}) collective-permute-start(bf16[128,1024]{1,0:T(8,128)(2,1)S(1)} %get-tuple-element.35), channel_id=1, source_target_pairs={{0,1},{1,0},{2,3},{3,2},{4,5},{5,4},{6,7},{7,6},{8,9},{9,8},{10,11... | collective-permute-start | bytes 786440 | tf_op jit(solution)/shard_map/ppermute | solution.py:30
  69.0 12.9 %collective-permute-start.6 = (bf16[128,1024]{1,0:T(8,128)(2,1)S(1)}, bf16[128,1024]{1,0:T(8,128)(2,1)S(1)}, u32[]{:S(2)}, u32[]{:S(2)}) collective-permute-start(bf16[128,1024]{1,0:T(8,128)(2,1)S(1)} %get-tuple-element.33), channel_id=1, source_target_pairs={{0,1},{1,0},{2,3},{3,2},{4,5},{5,4},{6,7},{7,6},{8,9},{9,8},{10,11... | collective-permute-start | bytes 786440 | tf_op jit(solution)/shard_map/ppermute | solution.py:30
  80.5 7.9 %collective-permute-start.8 = (bf16[128,1024]{1,0:T(8,128)(2,1)S(1)}, bf16[128,1024]{1,0:T(8,128)(2,1)S(1)}, u32[]{:S(2)}, u32[]{:S(2)}) collective-permute-start(bf16[128,1024]{1,0:T(8,128)(2,1)S(1)} %broadcast_select_fusion.2), channel_id=1, source_target_pairs={{0,1},{1,0},{2,3},{3,2},{4,5},{5,4},{6,7},{7,6},{8,9},{9,8},{10,11... | collective-permute-start | bytes 786440 | tf_op jit(solution)/shard_map/ppermute | solution.py:30
  101.8 1.4 copy-start.4
  103.3 1.2 copy-start.9
  113.9 4.1 %copy-start.3 = (bf16[512,2048]{1,0:T(8,128)(2,1)S(1)}, bf16[512,2048]{1,0:T(8,128)(2,1)}, u32[]{:S(2)}) copy-start(bf16[512,2048]{1,0:T(8,128)(2,1)} %copy-done.2) | copy-start | bytes 6291460
  117.9 8.9 %copy-start.7 = (bf16[512,1536]{1,0:T(8,128)(2,1)}, bf16[512,1536]{1,0:T(8,128)(2,1)S(1)}, u32[]{:S(2)}) copy-start(bf16[512,1536]{1,0:T(8,128)(2,1)S(1)} %multiply_convert_fusion.3.pre_ref) | copy-start | bytes 4718596
  130.7 64.2 %dynamic-slice-start = ((f32[2048]{0:T(1024)}, s32[]{:T(128)}), f32[1024]{0:T(1024)S(1)}, s32[]{:S(2)}) async-start(f32[2048]{0:T(1024)} %param.11, s32[]{:T(128)} %select_n.101), calls=%async_computation | async-start | bytes 8704 | tf_op jit(solution)/shard_map/dynamic-slice
  194.9 5.2 %copy-start.1 = (bf16[512,2048]{1,0:T(8,128)(2,1)S(1)}, bf16[512,2048]{1,0:T(8,128)(2,1)}, u32[]{:S(2)}) copy-start(bf16[512,2048]{1,0:T(8,128)(2,1)} %param.13) | copy-start | bytes 6291460
  194.9 4.4 %copy-start.10 = (f32[128,1536]{1,0:T(8,128)S(1)}, f32[128,1536]{1,0:T(8,128)}, u32[]{:S(2)}) copy-start(f32[128,1536]{1,0:T(8,128)} %get-tuple-element.66) | copy-start | bytes 2359300

commit v2 on v1

--- a/solution.py
+++ b/solution.py
@@ -25,13 +25,7 @@
 
 
 def gathered(block):
-    if lax.axis_size("mp") != 2:
-        return lax.all_gather(block, "mp", axis=1, tiled=True)
-    other = lax.ppermute(block, "mp", [(0, 1), (1, 0)])
-    first = lax.axis_index("mp") == 0
-    return jnp.concatenate(
-        [jnp.where(first, block, other), jnp.where(first, other, block)], axis=1
-    )
+    return lax.all_gather(block, "mp", axis=1, tiled=True)
 
 
 def forward_heads(acts, visible, heads_here):
@@ -312,30 +306,139 @@
     )(normed, grad_pre, full_dy, mixed, term, sums)
 
 
+def gather_kernel(
+    x_ref, moved_ref, flags_ref, gain_ref, w_ref,
+    fullx_ref, fully_ref, normed_ref, pre_ref, mean_ref, inv_ref,
+    land_z, land_x, land_y, chosen,
+    sem_zs, sem_zr, sem_xs, sem_xr, sem_ys, sem_yr,
+):
+    d = lax.axis_index("dp")
+    m = lax.axis_index("mp")
+    half = x_ref.shape[1]
+    partner = (d + 8) % 16
+    barrier = pltpu.get_barrier_semaphore()
+    pl.semaphore_signal(barrier, inc=1, device_id={"dp": partner}, device_id_type=MESH)
+    pl.semaphore_signal(barrier, inc=1, device_id={"mp": 1 - m}, device_id_type=MESH)
+    pl.semaphore_wait(barrier, 2)
+    here = pl.ds(pl.multiple_of(m * half, half), half)
+    there = pl.ds(pl.multiple_of((1 - m) * half, half), half)
+
+    def rows_of(j):
+        return pl.ds(pl.multiple_of(j * BLOCK, BLOCK), BLOCK)
+
+    def swap_rows(j):
+        return pltpu.make_async_remote_copy(
+            src_ref=moved_ref.at[rows_of(j)], dst_ref=land_z.at[j],
+            send_sem=sem_zs.at[j], recv_sem=sem_zr.at[j],
+            device_id={"dp": partner}, device_id_type=MESH,
+        )
+
+    def share_x(j):
+        return pltpu.make_async_remote_copy(
+            src_ref=x_ref.at[rows_of(j)], dst_ref=land_x.at[j],
+            send_sem=sem_xs.at[j], recv_sem=sem_xr.at[j],
+            device_id={"mp": 1 - m}, device_id_type=MESH,
+        )
+
+    def share_y(j):
+        return pltpu.make_async_remote_copy(
+            src_ref=chosen.at[j], dst_ref=land_y.at[j],
+            send_sem=sem_ys.at[j], recv_sem=sem_yr.at[j],
+            device_id={"mp": 1 - m}, device_id_type=MESH,
+        )
+
+    def begin(j, carry):
+        swap_rows(j).start()
+        share_x(j).start()
+        return carry
+
+    def block(j, carry):
+        rows = rows_of(j)
+        share_x(j).wait_recv()
+        fullx_ref[rows, here] = x_ref[rows, :]
+        fullx_ref[rows, there] = land_x[j]
+        wide = fullx_ref[rows, :].astype(jnp.float32)
+        mean = jnp.mean(wide, axis=1, keepdims=True)
+        shifted = wide - mean
+        inverse = lax.rsqrt(jnp.mean(shifted * shifted, axis=1, keepdims=True) + epsilon)
+        mean_ref[rows, :] = mean
+        inv_ref[rows, :] = inverse
+        normed = (shifted * inverse * gain_ref[...]).astype(jnp.bfloat16)
+        normed_ref[rows, :] = normed
+        pre_ref[rows, :] = jnp.dot(normed, w_ref[...], preferred_element_type=jnp.float32)
+        swap_rows(j).wait_recv()
+        chosen[j] = jnp.where(
+            flags_ref[rows, :] == 1,
+            land_z[j].astype(jnp.float32),
+            moved_ref[rows, :].astype(jnp.float32),
+        ).astype(jnp.bfloat16)
+        share_y(j).start()
+        fully_ref[rows, here] = chosen[j]
+        return carry
+
+    def finish(j, carry):
+        share_y(j).wait_recv()
+        fully_ref[rows_of(j), there] = land_y[j]
+        swap_rows(j).wait_send()
+        share_x(j).wait_send()
+        share_y(j).wait_send()
+        return carry
+
+    lax.fori_loop(0, 4, begin, 0)
+    lax.fori_loop(0, 4, block, 0)
+    lax.fori_loop(0, 4, finish, 0)
+
+
+def gathered_rows(inputs, grad_moved, moved, gain, proj_in):
+    rows, half = inputs.shape
+    low, full = jnp.bfloat16, jnp.float32
+    flags = jnp.repeat(moved[0], BLOCK)[:, None]
+    landing = pltpu.VMEM((4, BLOCK, half), low)
+    return pl.pallas_call(
+        gather_kernel,
+        out_shape=(
+            jax.ShapeDtypeStruct((rows, 2 * half), low),
+            jax.ShapeDtypeStruct((rows, 2 * half), low),
+            jax.ShapeDtypeStruct((rows, 2 * half), low),
+            jax.ShapeDtypeStruct((rows, proj_in.shape[1]), full),
+            jax.ShapeDtypeStruct((rows, 1), full),
+            jax.ShapeDtypeStruct((rows, 1), full),
+        ),
+        in_specs=[pl.BlockSpec(memory_space=pltpu.VMEM)] * 5,
+        out_specs=[pl.BlockSpec(memory_space=pltpu.VMEM)] * 6,
+        scratch_shapes=[landing] * 4 + [pltpu.SemaphoreType.DMA((4,))] * 6,
+        compiler_params=pltpu.CompilerParams(
+            collective_id=1, has_side_effects=True, vmem_limit_bytes=48 * 1024 * 1024
+        ),
+    )(inputs, grad_moved, flags, gain[None, :], proj_in)
+
+
 def on_device(inputs, grad_moved, moved, segments, input_norm_gain, proj_in, proj_out):
     rows = inputs.shape[0]
     span = 2 * DV + 2 * DQK
     heads_here = proj_in.shape[1] // span
-    top_bit = lax.axis_size("dp").bit_length() - 2
-    blocks = rows // BLOCK
-    mine = [grad_moved[j * BLOCK : (j + 1) * BLOCK] for j in range(blocks)]
-    theirs = [swapped(block, "dp", top_bit) for block in mine]
-    full_x = gathered(inputs)
-    after, returned = full_x, []
-    for j in range(blocks):
-        landed, after = lax.optimization_barrier((theirs[j], after))
-        full_x = after if j == 0 else full_x
-        after = jnp.where(moved[0, j] == 1, landed, mine[j])
-        returned.append(gathered(after))
-    full_dy = jnp.concatenate(returned, axis=0)
-    xfull = full_x.astype(jnp.float32)
-    mean_shifted = xfull - jnp.mean(xfull, axis=1, keepdims=True)
-    inverse_deviation = lax.rsqrt(
-        jnp.mean(mean_shifted * mean_shifted, axis=1, keepdims=True) + epsilon
-    )
-    standardized_input = mean_shifted * inverse_deviation
-    normalized_rows = (standardized_input * input_norm_gain[None, :]).astype(jnp.bfloat16)
-    pre = jnp.dot(normalized_rows, proj_in, preferred_element_type=jnp.float32)
+    if lax.axis_size("mp") == 2 and lax.axis_size("dp") == 16:
+        full_x, full_dy, normalized_rows, pre, row_mean, inverse_deviation = gathered_rows(
+            inputs, grad_moved, moved, input_norm_gain, proj_in
+        )
+        standardized_input = (full_x.astype(jnp.float32) - row_mean) * inverse_deviation
+    else:
+        top_bit = lax.axis_size("dp").bit_length() - 2
+        blocks = rows // BLOCK
+        mine = [grad_moved[j * BLOCK : (j + 1) * BLOCK] for j in range(blocks)]
+        theirs = [swapped(block, "dp", top_bit) for block in mine]
+        full_x = gathered(inputs)
+        full_dy = jnp.concatenate(
+            [gathered(jnp.where(moved[0, j] == 1, theirs[j], mine[j])) for j in range(blocks)], axis=0
+        )
+        xfull = full_x.astype(jnp.float32)
+        mean_shifted = xfull - jnp.mean(xfull, axis=1, keepdims=True)
+        inverse_deviation = lax.rsqrt(
+            jnp.mean(mean_shifted * mean_shifted, axis=1, keepdims=True) + epsilon
+        )
+        standardized_input = mean_shifted * inverse_deviation
+        normalized_rows = (standardized_input * input_norm_gain[None, :]).astype(jnp.bfloat16)
+        pre = jnp.dot(normalized_rows, proj_in, preferred_element_type=jnp.float32)
     sig_p = jax.nn.sigmoid(pre)
     acts = (pre * sig_p).astype(jnp.bfloat16)
     grad_mix = lax.dot_general(

time: 201 us -> 179 us (0.89)
  Pallas kernels: 61.7 us -> 125 us
  waiting for transfers between devices: 49.8 us -> 0 us
  other arithmetic: 31.7 us -> 17.3 us
  starting transfers between devices: 13.7 us -> 0 us
  matrix products: 23.1 us -> 17.5 us
  between operations: 3.41 us -> 0.87 us
    pallas_call x0 -> x1, Pallas kernels: none -> 63.1 us  [gathered_rows(): pl.pallas_call(gather_kernel, out_shape=(jax.ShapeDtypeStruct((rows, 2 *...]
    ppermute x9 -> x0, waiting for transfers between devices: 49.8 us -> none  [the longest x4 30.1 us: swapped(): return lax.ppermute(block, axis, route)]
    ppermute x9 -> x0, starting transfers between devices: 13.7 us -> none  [the longest x5 8.11 us: gathered(): other = lax.ppermute(block, 'mp', [(0, 1), (1, 0)])]
    concatenate x2 -> x0, other arithmetic: 13.5 us -> none  [the longest x1 13.4 us: on_device(): full_dy = jnp.concatenate(returned, axis=0)]
    dot_general x1 -> x0, matrix products: 5.33 us -> none  [on_device(): pre = jnp.dot(normalized_rows, proj_in, preferred_element_type=jnp.float32)]
    convert_element_type x1, other arithmetic: 0.69 us -> 4.23 us  [on_device(): acts = (pre * sig_p).astype(jnp.bfloat16)]
    unnamed x30 -> x32, local copies, waits for them, and re-layouts: 4.09 us -> 7.38 us
    slice x2 -> x0, local copies, waits for them, and re-layouts: 3.07 us -> none  [the longest x1 1.67 us: on_device(): mine = [grad_moved[j * BLOCK:(j + 1) * BLOCK] for j in range(blocks)]]
  transfers between devices with their start and end apart: 9 -> 0, of which waited for: 5 -> 0; matrix products, arithmetic and copies ran while one was open for 5% -> 0% of each run, Pallas kernels for 0% -> 0%
where the time goes in v2:
time: 179 us; the launch traced here: 178 us
  Pallas kernels  125 us (70%)
  local copies, waits for them, and re-layouts  17.9 us (10%)
  matrix products  17.5 us (10%)
  other arithmetic  17.3 us (10%)
    pallas_call x1, Pallas kernels, gathered_rows(): pl.pallas_call(gather_kernel, out_shape=(jax.ShapeDtypeStruct((rows, 2 *...  63.1 us
    pallas_call x1, Pallas kernels, reduced(): pl.pallas_call(reduce_kernel, out_shape=(jax.ShapeDtypeStruct((128, wide)...  61.9 us
    dot_general x1, matrix products, on_device(): lax.dot_general(grad_pre, proj_in, (((1,), (1,)), ((), ())), preferred_el...  8.89 us
    unnamed x32, local copies, waits for them, and re-layouts  7.38 us
    convert_element_type x1, other arithmetic, on_device(): input_gradient = grad_here.astype(jnp.bfloat16)  4.29 us
    convert_element_type x1, other arithmetic, on_device(): acts = (pre * sig_p).astype(jnp.bfloat16)  4.23 us
    convert_element_type x1, other arithmetic, on_device(): (grad_act * sig_p * (1.0 + pre * (1.0 - sig_p))).astype(jnp.bfloat16)  4.08 us
    reshape x1, local copies, waits for them, and re-layouts, backward_heads(): return grad_act.reshape(rows, heads_here * (2 * DV + 2 * DQK))  3.58 us

profile of v2, /device:TPU:0, one launch (start us, length us, event | category | flops | bytes accessed | tf_op | source)
XLA Modules:
  0.0 178.5 jit_solution(4854648211805145391)
XLA Ops:
  0.6 0.9 broadcast_in_dim.4
  1.7 1.2 copy-done.1
  2.9 1.2 copy-done.2
  4.1 0.7 copy-done.3
  4.8 63.1 %shard_map.94 = (bf16[512,2048]{1,0:T(8,128)(2,1)S(1)}, bf16[512,2048]{1,0:T(8,128)(2,1)}, bf16[512,2048]{1,0:T(8,128)(2,1)}, f32[512,1536]{1,0:T(8,128)}, f32[512,1]{1,0:T(8,128)S(1)}, /*index=5*/f32[512,1]{1,0:T(8,128)S(1)}) custom-call(bf16[512,1024]{1,0:T(8,128)(2,1)S(1)} %copy-done.1, bf16[512,1024]{1,0:T(8,128)(2,1)S(1)} %copy-done.2, ...), custom_call_target="tpu_custom_call" | custom-call | tf_op jit(solution)/shard_map/pallas_call | solution.py:397
  67.9 1.3 copy-done.5
  69.7 4.2 %multiply_convert_fusion.3 = bf16[512,1536]{1,0:T(8,128)(2,1)} fusion(f32[512,1536]{1,0:T(8,128)} %get-tuple-element.15), kind=kLoop, calls=%fused_computation.9 | loop fusion | flops 3932160 | bytes 4718592 | tf_op jit(solution)/shard_map/convert_element_type | solution.py:443
  73.9 2.6 %copy.33 = bf16[512,1536]{0,1:T(8,128)(2,1)} copy(bf16[512,1536]{1,0:T(8,128)(2,1)} %multiply_convert_fusion.3) | data formatting | bytes 3145728 | tf_op jit(solution)/shard_map/reshape | solution.py:34
  76.6 2.7 %multiply_convert_fusion.1 = (bf16[4,512,512]{2,1,0:T(8,128)(2,1)S(1)}, f32[4,512,512]{2,1,0:T(8,128)S(1)}) fusion(f32[512,512]{1,0:T(8,128)S(1)} %fusion.3, bf16[512,4,384]{0,2,1:T(8,128)(2,1)} %bitcast.36), kind=kOutput, calls=%fused_computation.5 | convolution fusion | flops 140509184 | bytes 7864320 | tf_op jit(solution)/shard_map/qhd,khd->hqk/dot_general | solution.py:39
  79.3 0.8 fusion.14
  80.1 0.7 copy-done.9
  80.9 1.4 fusion.15
  83.6 2.1 %multiply_convert_fusion = bf16[4,512,512]{2,1,0:T(8,128)(2,1)S(1)} fusion(f32[4,512,512]{2,1,0:T(8,128)S(1)} %get-tuple-element.39, bf16[512,4,128]{0,2,1:T(8,128)(2,1)S(1)} %multiply_convert_fusion.4, f32[512,512]{1,0:T(8,128)S(1)} %copy-done.11, bf16[512,4,384]{0,2,1:T(8,128)(2,1)S(1)} %bitcast.40), kind=kOutput, calls=%fused_computation.4 | convolution fusion | flops 278921216 | bytes 8388608 | tf_op jit(solution)/shard_map/qhd,khd->hqk/dot_general | solution.py:66
  86.2 0.7 convolution_bitcast_fusion.3
  87.4 2.0 %pad_maximum_fusion = f32[512,4,384]{0,2,1:T(8,128)} fusion(f32[512,4,64]{0,2,1:T(8,128)S(1)} %convolution_bitcast_fusion.2, f32[512,4,64]{0,2,1:T(8,128)S(1)} %convolution_bitcast_fusion.3, f32[512,4,128]{0,2,1:T(8,128)S(1)} %convolution_bitcast_fusion, f32[512,4,128]{0,2,1:T(8,128)S(1)} %get-tuple-element.35), kind=kLoop, calls=%fused_computation.7 | loop fusion | flops 2359296 | bytes 6291456 | tf_op jit(solution)/shard_map/concatenate | solution.py:71
  89.4 3.6 %copy.31 = f32[512,1536]{1,0:T(8,128)} copy(f32[512,1536]{0,1:T(8,128)} %bitcast.35) | data formatting | bytes 6291456 | tf_op jit(solution)/shard_map/reshape | solution.py:72
  93.0 4.1 %multiply_convert_fusion.2.pre_ref = bf16[512,1536]{1,0:T(8,128)(2,1)S(1)} fusion(f32[512,1536]{1,0:T(8,128)} %get-tuple-element.15, f32[512,1536]{1,0:T(8,128)} %copy.31), kind=kLoop, calls=%fused_computation.8 | loop fusion | flops 7077888 | bytes 7864320 | tf_op jit(solution)/shard_map/convert_element_type | solution.py:453
  97.1 8.9 %fusion = (f32[512]{0:T(512)S(1)}, f32[512]{0:T(512)S(1)}, f32[512,2048]{1,0:T(8,128)}, bf16[512,2048]{1,0:T(8,128)(2,1)}) fusion(f32[2048]{0:T(1024)S(1)} %copy-done.4, f32[512]{0:T(512)S(1)} %reduce, f32[512]{0:T(512)S(1)} %reduce.1, bf16[512,2048]{1,0:T(8,128)(2,1)S(1)} %copy-done.6, bf16[512,1536]{1,0:T(8,128)(2,1)S(1)} %multiply_convert_fusion.2.pre_ref, ...), kind=kOutput, calls=%fused_computation.3 | convolution fusion | flops 3230661632 | bytes 16269312 | tf_op jit(solution)/shard_map/dot_general | solution.py:456
  106.0 1.0 copy.32.mixed_ref
  107.0 2.3 %constant_dynamic-slice_fusion.term_ref = bf16[512,1024]{1,0:T(8,128)(2,1)} fusion(bf16[512,2048]{1,0:T(8,128)(2,1)} %get-tuple-element.42, s32[]{:T(128)S(6)} %select_n.10), kind=kLoop, calls=%fused_computation.42 | loop fusion | bytes 2097156 | tf_op jit(solution)/shard_map/dynamic_slice | solution.py:462
  109.8 61.9 %shard_map.95 = (f32[128,1536]{1,0:T(8,128)}, f32[128,512]{1,0:T(8,128)}, bf16[512,1024]{1,0:T(8,128)(2,1)}, f32[2,512]{1,0:T(2,128)}) custom-call(bf16[512,2048]{1,0:T(8,128)(2,1)} %get-tuple-element.16.normed_ref, bf16[512,1536]{1,0:T(8,128)(2,1)} %copy-done.8, bf16[512,2048]{1,0:T(8,128)(2,1)} %get-tuple-element.13.dy_ref, ...), custom_call_target="tpu_custom_call" | custom-call | tf_op jit(solution)/shard_map/pallas_call | solution.py:271
  172.5 4.3 %add_convert_fusion = bf16[512,1024]{1,0:T(8,128)(2,1)} fusion(f32[512,2048]{1,0:T(8,128)} %get-tuple-element.34, s32[]{:T(128)S(6)} %select_n.4, bf16[512,1024]{1,0:T(8,128)(2,1)} %get-tuple-element.19, f32[512]{0:T(512)S(1)} %bitcast.47, f32[512]{0:T(512)S(1)} %bitcast.46, f32[1024]{0:T(1024)S(1)} %dynamic-slice.3, ...), kind=kLoop, calls=%fused_computation.12 | loop fusion | flops 5767168 | bytes 6301700 | tf_op jit(solution)/shard_map/convert_element_type | solution.py:494
  176.8 0.8 copy.28
  177.6 0.9 copy.35
  (41 shorter events, 4.3 us)
Async XLA Ops:
  0.6 79.5 %copy-start = (bf16[512,2048]{1,0:T(8,128)(2,1)S(1)}, bf16[512,2048]{1,0:T(8,128)(2,1)}, u32[]{:S(2)}) copy-start(bf16[512,2048]{1,0:T(8,128)(2,1)} %param.13) | copy-start | bytes 6291460
  1.7 1.2 copy-start.1
  2.9 1.2 copy-start.2
  4.1 0.7 copy-start.3
  4.8 64.7 %copy-start.14 = (s32[512]{0:T(512)S(1)}, s32[512]{0:T(512)}, u32[]{:S(2)}) copy-start(s32[512]{0:T(512)} %param.10) | copy-start | bytes 6148
  67.9 1.3 copy-start.5
  69.7 6.9 %copy-start.10 = (f32[512,512]{1,0:T(8,128)}, f32[512,512]{1,0:T(8,128)S(1)}, u32[]{:S(2)}) copy-start(f32[512,512]{1,0:T(8,128)S(1)} %fusion.3) | copy-start | bytes 3145732
  76.6 2.7 %copy-start.7 = (bf16[512,1536]{0,1:T(8,128)(2,1)S(1)}, bf16[512,1536]{0,1:T(8,128)(2,1)}, u32[]{:S(2)}) copy-start(bf16[512,1536]{0,1:T(8,128)(2,1)} %copy.33) | copy-start | bytes 4718596
  79.3 1.6 copy-start.9
  82.4 1.2 copy-start.11
  93.0 4.1 %copy-start.4 = (f32[2048]{0:T(1024)S(1)}, f32[2048]{0:T(1024)}, u32[]{:S(2)}) copy-start(f32[2048]{0:T(1024)} %param.11) | copy-start | bytes 24580
  93.0 4.1 %copy-start.6 = (bf16[512,2048]{1,0:T(8,128)(2,1)S(1)}, bf16[512,2048]{1,0:T(8,128)(2,1)}, u32[]{:S(2)}) copy-start(bf16[512,2048]{1,0:T(8,128)(2,1)} %copy-done.5) | copy-start | bytes 6291460
  97.1 8.9 %copy-start.8 = (bf16[512,1536]{1,0:T(8,128)(2,1)}, bf16[512,1536]{1,0:T(8,128)(2,1)S(1)}, u32[]{:S(2)}) copy-start(bf16[512,1536]{1,0:T(8,128)(2,1)S(1)} %multiply_convert_fusion.2.pre_ref) | copy-start | bytes 4718596
  172.5 4.3 %copy-start.13 = (f32[128,512]{1,0:T(8,128)S(1)}, f32[128,512]{1,0:T(8,128)}, u32[]{:S(2)}) copy-start(f32[128,512]{1,0:T(8,128)} %get-tuple-element.22) | copy-start | bytes 786436
  172.5 5.1 %copy-start.12 = (f32[128,1536]{1,0:T(8,128)S(1)}, f32[128,1536]{1,0:T(8,128)}, u32[]{:S(2)}) copy-start(f32[128,1536]{1,0:T(8,128)} %get-tuple-element.49) | copy-start | bytes 2359300

commit v3 on v2

--- a/solution.py
+++ b/solution.py
@@ -76,9 +76,10 @@
 
 
 def reduce_kernel(
-    normed_ref, pre_ref, dy_ref, mixed_ref, term_ref, sums_ref,
-    gin_ref, gout_ref, rterm_ref, rsums_ref,
+    normed_ref, pre_ref, dy_ref, mixed_ref, w_ref, x_ref, mean_ref, inv_ref, gain_ref,
+    gin_ref, gout_ref, grad_ref,
     own, send_c, recv_c, send_y, recv_y, keep_y, send_z, from_low, from_high, land_t, land_s,
+    send_t, send_s, own_t,
     sem_cs, sem_cr, sem_ys, sem_yr, sem_zs, sem_low, sem_high, sem_xs, sem_xr,
 ):
     wide = pre_ref.shape[1]
@@ -117,10 +118,64 @@
             device_id=where, device_id_type=MESH,
         )
 
-    cross_t = remote(term_ref, land_t, sem_xs.at[0], sem_xr.at[0], {"mp": 1 - x})
-    cross_s = remote(sums_ref, land_s, sem_xs.at[1], sem_xr.at[1], {"mp": 1 - x})
-    cross_t.start()
-    cross_s.start()
+    half = land_t.shape[1]
+
+    def part(side):
+        return pl.ds(pl.multiple_of(side * half, half), half)
+
+    def rows_of(j):
+        return pl.ds(pl.multiple_of(j * 128, 128), 128)
+
+    def cross_t(j):
+        rows = rows_of(j)
+        return remote(
+            send_t.at[rows], land_t.at[rows], sem_xs.at[j], sem_xr.at[j], {"mp": 1 - x}
+        )
+
+    cross_s = remote(send_s, land_s, sem_xs.at[4], sem_xr.at[4], {"mp": 1 - x})
+
+    def standard(rows, side):
+        wide_x = x_ref[rows, part(side)].astype(jnp.float32)
+        return (wide_x - mean_ref[rows, :]) * inv_ref[rows, :]
+
+    def terms(j, carry):
+        rows = rows_of(j)
+
+        def half_term(side):
+            term = lax.dot_general(
+                pre_ref[rows, :], w_ref[part(side), :], (((1,), (1,)), ((), ())),
+                preferred_element_type=jnp.float32,
+            ).astype(jnp.bfloat16)
+            scaled = term.astype(jnp.float32) * gain_ref[:, part(side)]
+            first = jnp.sum(scaled, axis=1, keepdims=True)
+            second = jnp.sum(scaled * standard(rows, side), axis=1, keepdims=True)
+            return term, first, second
+
+        away, first_a, second_a = half_term(1 - x)
+        send_t[rows, :] = away
+        cross_t(j).start()
+        kept, first_k, second_k = half_term(x)
+        own_t[rows, :] = kept
+        lane = lax.broadcasted_iota(jnp.int32, (128, 128), 1)
+        send_s[rows, :] = jnp.where(lane == 0, first_a + first_k, second_a + second_k)
+        return carry
+
+    def gradient(j, carry):
+        rows = rows_of(j)
+        cross_t(j).wait_recv()
+        means = (send_s[rows, :] + land_s[rows, :]) * (1.0 / (2 * half))
+        normed_grad = own_t[rows, :].astype(jnp.float32) + land_t[rows, :].astype(jnp.float32)
+        grad_ref[rows, :] = (
+            dy_ref[rows, part(x)].astype(jnp.float32)
+            + inv_ref[rows, :]
+            * (
+                normed_grad * gain_ref[:, part(x)]
+                - means[:, 0:1]
+                - standard(rows, x) * means[:, 1:2]
+            )
+        ).astype(jnp.bfloat16)
+        cross_t(j).wait_send()
+        return carry
 
     def target(k):
         v = (3 - k) + (k // 2) * inner * (2 * k - 5)
@@ -179,6 +234,8 @@
         return carry
 
     lax.fori_loop(0, 8, step, 0)
+    lax.fori_loop(0, 4, terms, 0)
+    cross_s.start()
 
     def up(k, t):
         return remote(send_z.at[k], from_low.at[t], sem_zs.at[k], sem_low.at[t], {"dp": d + 4})
@@ -223,6 +280,8 @@
         return carry
 
     lax.fori_loop(0, 4, along, 0)
+    cross_s.wait()
+    lax.fori_loop(0, 4, gradient, 0)
 
     @pl.when(z > 0)
     def _():
@@ -236,10 +295,6 @@
 
     gin_ref[...] = own[:, :wide]
     gout_ref[...] = own[:, wide:]
-    cross_t.wait()
-    cross_s.wait()
-    rterm_ref[...] = land_t[...]
-    rsums_ref[...] = land_s[...]
 
     def drain(slot, carry):
         to_core(slot).wait_send()
@@ -264,7 +319,8 @@
     lax.fori_loop(0, 4, drain_far, 0)
 
 
-def reduced(normed, grad_pre, full_dy, mixed, term, sums):
+def reduced(normed, grad_pre, full_dy, mixed, proj_in, full_x, mean, inverse, gain):
+    rows, half = full_x.shape[0], full_x.shape[1] // 2
     wide, narrow = grad_pre.shape[1], mixed.shape[1]
     total = wide + narrow
     low, full = jnp.bfloat16, jnp.float32
@@ -273,11 +329,10 @@
         out_shape=(
             jax.ShapeDtypeStruct((128, wide), full),
             jax.ShapeDtypeStruct((128, narrow), full),
-            jax.ShapeDtypeStruct(term.shape, low),
-            jax.ShapeDtypeStruct(sums.shape, full),
+            jax.ShapeDtypeStruct((rows, half), low),
         ),
-        in_specs=[pl.BlockSpec(memory_space=pltpu.VMEM)] * 6,
-        out_specs=[pl.BlockSpec(memory_space=pltpu.VMEM)] * 4,
+        in_specs=[pl.BlockSpec(memory_space=pltpu.VMEM)] * 9,
+        out_specs=[pl.BlockSpec(memory_space=pltpu.VMEM)] * 3,
         scratch_shapes=[
             pltpu.VMEM((128, total), full),
             pltpu.VMEM((8, 128, total), low),
@@ -288,8 +343,11 @@
             pltpu.VMEM((4, 128, total), low),
             pltpu.VMEM((4, 128, total), low),
             pltpu.VMEM((4, 128, total), low),
-            pltpu.VMEM(term.shape, low),
-            pltpu.VMEM(sums.shape, full),
+            pltpu.VMEM((rows, half), low),
+            pltpu.VMEM((rows, 128), full),
+            pltpu.VMEM((rows, half), low),
+            pltpu.VMEM((rows, 128), full),
+            pltpu.VMEM((rows, half), low),
             pltpu.SemaphoreType.DMA((8,)),
             pltpu.SemaphoreType.DMA((8,)),
             pltpu.SemaphoreType.DMA((4,)),
@@ -297,13 +355,13 @@
             pltpu.SemaphoreType.DMA((4,)),
             pltpu.SemaphoreType.DMA((4,)),
             pltpu.SemaphoreType.DMA((4,)),
-            pltpu.SemaphoreType.DMA((2,)),
-            pltpu.SemaphoreType.DMA((2,)),
+            pltpu.SemaphoreType.DMA((5,)),
+            pltpu.SemaphoreType.DMA((5,)),
         ],
         compiler_params=pltpu.CompilerParams(
             collective_id=0, has_side_effects=True, vmem_limit_bytes=60 * 1024 * 1024
         ),
-    )(normed, grad_pre, full_dy, mixed, term, sums)
+    )(normed, grad_pre, full_dy, mixed, proj_in, full_x, mean, inverse, gain[None, :])
 
 
 def gather_kernel(
@@ -413,6 +471,78 @@
     )(inputs, grad_moved, flags, gain[None, :], proj_in)
 
 
+def heads_kernel(pre_ref, dy_ref, w_ref, seg_col_ref, seg_row_ref, grad_ref, mixed_ref):
+    low, full = jnp.bfloat16, jnp.float32
+    pre = pre_ref[...]
+    sig_p = jax.nn.sigmoid(pre)
+    act = (pre * sig_p).astype(low)
+    slope_p = sig_p * (1.0 + pre * (1.0 - sig_p))
+    u_vals = act[:, :DV].astype(full)
+    v_vals = act[:, DV : 2 * DV]
+    q_vals = act[:, 2 * DV : 2 * DV + DQK]
+    k_vals = act[:, 2 * DV + DQK :]
+
+    def dot(a, b, i, j):
+        return lax.dot_general(a, b, (((i,), (j,)), ((), ())), preferred_element_type=full)
+
+    scores = dot(q_vals, k_vals, 1, 1)
+    shape = scores.shape
+    row = lax.broadcasted_iota(jnp.int32, shape, 0)
+    col = lax.broadcasted_iota(jnp.int32, shape, 1)
+    visible = jnp.where((seg_col_ref[...] == seg_row_ref[...]) & (col <= row), 1.0, 0.0)
+    sig_s = jax.nn.sigmoid(scores)
+    attend = (scores * sig_s * visible).astype(low)
+    slope = sig_s * (1.0 + scores * (1.0 - sig_s)) * visible
+    outvals = dot(attend, v_vals, 1, 0)
+    shifted = outvals - jnp.mean(outvals, axis=1, keepdims=True)
+    head_inv = lax.rsqrt(jnp.mean(shifted * shifted, axis=1, keepdims=True) + head_floor)
+    onorm = shifted * head_inv
+    mixed_ref[...] = (onorm * u_vals).astype(low)
+    grad_mix = dot(dy_ref[...], w_ref[...], 1, 1)
+    gon = grad_mix * u_vals
+    grad_o = (
+        head_inv
+        * (
+            gon
+            - jnp.mean(gon, axis=1, keepdims=True)
+            - onorm * jnp.mean(gon * onorm, axis=1, keepdims=True)
+        )
+    ).astype(low)
+    grad_scores = (dot(grad_o, v_vals, 1, 1) * slope).astype(low)
+    grad_ref[:, :DV] = (grad_mix * onorm * slope_p[:, :DV]).astype(low)
+    grad_ref[:, DV : 2 * DV] = (dot(attend, grad_o, 0, 0) * slope_p[:, DV : 2 * DV]).astype(low)
+    grad_qk = jnp.concatenate(
+        [dot(grad_scores, k_vals, 1, 0), dot(grad_scores, q_vals, 0, 0)], axis=1
+    )
+    grad_ref[:, 2 * DV :] = (grad_qk * slope_p[:, 2 * DV :]).astype(low)
+
+
+def heads_pass(pre, full_dy, proj_out, segments):
+    rows, width = pre.shape
+    span = 2 * DV + 2 * DQK
+    heads_here = width // span
+    return pl.pallas_call(
+        heads_kernel,
+        grid=(heads_here,),
+        out_shape=(
+            jax.ShapeDtypeStruct((rows, width), jnp.bfloat16),
+            jax.ShapeDtypeStruct((rows, heads_here * DV), jnp.bfloat16),
+        ),
+        in_specs=[
+            pl.BlockSpec((rows, span), lambda h: (0, h)),
+            pl.BlockSpec(full_dy.shape, lambda h: (0, 0)),
+            pl.BlockSpec((DV, proj_out.shape[1]), lambda h: (h, 0)),
+            pl.BlockSpec((rows, 1), lambda h: (0, 0)),
+            pl.BlockSpec((1, rows), lambda h: (0, 0)),
+        ],
+        out_specs=[
+            pl.BlockSpec((rows, span), lambda h: (0, h)),
+            pl.BlockSpec((rows, DV), lambda h: (0, h)),
+        ],
+        compiler_params=pltpu.CompilerParams(vmem_limit_bytes=40 * 1024 * 1024),
+    )(pre, full_dy, proj_out, segments[:, None], segments[None, :])
+
+
 def on_device(inputs, grad_moved, moved, segments, input_norm_gain, proj_in, proj_out):
     rows = inputs.shape[0]
     span = 2 * DV + 2 * DQK
@@ -421,24 +551,28 @@
         full_x, full_dy, normalized_rows, pre, row_mean, inverse_deviation = gathered_rows(
             inputs, grad_moved, moved, input_norm_gain, proj_in
         )
-        standardized_input = (full_x.astype(jnp.float32) - row_mean) * inverse_deviation
-    else:
-        top_bit = lax.axis_size("dp").bit_length() - 2
-        blocks = rows // BLOCK
-        mine = [grad_moved[j * BLOCK : (j + 1) * BLOCK] for j in range(blocks)]
-        theirs = [swapped(block, "dp", top_bit) for block in mine]
-        full_x = gathered(inputs)
-        full_dy = jnp.concatenate(
-            [gathered(jnp.where(moved[0, j] == 1, theirs[j], mine[j])) for j in range(blocks)], axis=0
-        )
-        xfull = full_x.astype(jnp.float32)
-        mean_shifted = xfull - jnp.mean(xfull, axis=1, keepdims=True)
-        inverse_deviation = lax.rsqrt(
-            jnp.mean(mean_shifted * mean_shifted, axis=1, keepdims=True) + epsilon
-        )
-        standardized_input = mean_shifted * inverse_deviation
-        normalized_rows = (standardized_input * input_norm_gain[None, :]).astype(jnp.bfloat16)
-        pre = jnp.dot(normalized_rows, proj_in, preferred_element_type=jnp.float32)
+        grad_pre, mixed = heads_pass(pre, full_dy, proj_out, segments)
+        grad_proj_in, grad_proj_out, input_gradient = reduced(
+            normalized_rows, grad_pre, full_dy, mixed, proj_in,
+            full_x, row_mean, inverse_deviation, input_norm_gain,
+        )
+        return (input_gradient, grad_proj_in, grad_proj_out.T)
+    top_bit = lax.axis_size("dp").bit_length() - 2
+    blocks = rows // BLOCK
+    mine = [grad_moved[j * BLOCK : (j + 1) * BLOCK] for j in range(blocks)]
+    theirs = [swapped(block, "dp", top_bit) for block in mine]
+    full_x = gathered(inputs)
+    full_dy = jnp.concatenate(
+        [gathered(jnp.where(moved[0, j] == 1, theirs[j], mine[j])) for j in range(blocks)], axis=0
+    )
+    xfull = full_x.astype(jnp.float32)
+    mean_shifted = xfull - jnp.mean(xfull, axis=1, keepdims=True)
+    inverse_deviation = lax.rsqrt(
+        jnp.mean(mean_shifted * mean_shifted, axis=1, keepdims=True) + epsilon
+    )
+    standardized_input = mean_shifted * inverse_deviation
+    normalized_rows = (standardized_input * input_norm_gain[None, :]).astype(jnp.bfloat16)
+    pre = jnp.dot(normalized_rows, proj_in, preferred_element_type=jnp.float32)
     sig_p = jax.nn.sigmoid(pre)
     acts = (pre * sig_p).astype(jnp.bfloat16)
     grad_mix = lax.dot_general(
@@ -458,32 +592,22 @@
     ).astype(jnp.bfloat16)
     term_scaled = normed_term.astype(jnp.float32) * input_norm_gain[None, :]
     sums = jnp.stack([jnp.sum(term_scaled, axis=1), jnp.sum(term_scaled * standardized_input, axis=1)])
-    if lax.axis_size("mp") == 2 and lax.axis_size("dp") == 16:
-        sent = lax.dynamic_slice_in_dim(normed_term, local - offset, local, 1)
-        kept = lax.dynamic_slice_in_dim(normed_term, offset, local, 1)
-        grad_proj_in, grad_proj_out, other_term, other_sums = reduced(
-            normalized_rows, grad_pre, full_dy, mixed, sent, sums
-        )
-        grad_proj_out = grad_proj_out.T
-        sums = sums + other_sums
-        grad_normed = kept.astype(jnp.float32) + other_term.astype(jnp.float32)
-    else:
-        partial_out = lax.dot_general(
-            mixed, full_dy, (((0,), (0,)), ((), ())), preferred_element_type=jnp.float32
-        )
-        grad_proj_out = lax.psum_scatter(
-            partial_out.astype(jnp.bfloat16), "dp", scatter_dimension=1, tiled=True
-        ).astype(jnp.float32)
-        partial_in = lax.dot_general(
-            normalized_rows, grad_pre, (((0,), (0,)), ((), ())), preferred_element_type=jnp.float32
-        )
-        grad_proj_in = lax.psum_scatter(
-            partial_in.astype(jnp.bfloat16), "dp", scatter_dimension=0, tiled=True
-        ).astype(jnp.float32)
-        sums = lax.psum(sums, "mp")
-        grad_normed = lax.psum_scatter(
-            normed_term, "mp", scatter_dimension=1, tiled=True
-        ).astype(jnp.float32)
+    partial_out = lax.dot_general(
+        mixed, full_dy, (((0,), (0,)), ((), ())), preferred_element_type=jnp.float32
+    )
+    grad_proj_out = lax.psum_scatter(
+        partial_out.astype(jnp.bfloat16), "dp", scatter_dimension=1, tiled=True
+    ).astype(jnp.float32)
+    partial_in = lax.dot_general(
+        normalized_rows, grad_pre, (((0,), (0,)), ((), ())), preferred_element_type=jnp.float32
+    )
+    grad_proj_in = lax.psum_scatter(
+        partial_in.astype(jnp.bfloat16), "dp", scatter_dimension=0, tiled=True
+    ).astype(jnp.float32)
+    sums = lax.psum(sums, "mp")
+    grad_normed = lax.psum_scatter(
+        normed_term, "mp", scatter_dimension=1, tiled=True
+    ).astype(jnp.float32)
     means = sums / standardized_input.shape[1]
     here = lambda array: lax.dynamic_slice_in_dim(array, offset, local, 1)
     grad_here = here(full_dy).astype(jnp.float32) + inverse_deviation * (

time: 179 us -> 162 us (0.905)
  Pallas kernels: 125 us -> 145 us
  matrix products: 17.5 us -> 0 us
  other arithmetic: 17.3 us -> 0 us
    dot_general x8 -> x0, matrix products: 17.5 us -> none  [the longest x1 8.89 us: on_device(): lax.dot_general(grad_pre, proj_in, (((1,), (1,)), ((), ())), preferred_el...]
    convert_element_type x5 -> x0, other arithmetic: 13.1 us -> none  [the longest x1 4.29 us: on_device(): input_gradient = grad_here.astype(jnp.bfloat16)]
    pallas_call x0 -> x1, Pallas kernels: none -> 12.1 us  [heads_pass(): pl.pallas_call(heads_kernel, grid=(heads_here,), out_shape=(jax.ShapeDtyp...]
    unnamed x32 -> x29, local copies, waits for them, and re-layouts: 7.38 us -> 15.1 us
    pallas_call x1, Pallas kernels: 61.9 us -> 69.3 us  [reduced(): pl.pallas_call(reduce_kernel, out_shape=(jax.ShapeDtypeStruct((128, wide)...]
    reshape x3 -> x0, local copies, waits for them, and re-layouts: 7.23 us -> none  [the longest x1 3.58 us: backward_heads(): return grad_act.reshape(rows, heads_here * (2 * DV + 2 * DQK))]
    dynamic_slice x1 -> x0, local copies, waits for them, and re-layouts: 2.26 us -> none  [on_device(): sent = lax.dynamic_slice_in_dim(normed_term, local - offset, local, 1)]
    concatenate x1 -> x0, other arithmetic: 2.01 us -> none  [backward_heads(): grad_act = jnp.concatenate([grad_u, grad_v, grad_q, grad_k], axis=-1)]
where the time goes in v3:
time: 162 us
  Pallas kernels  145 us (90%)
  local copies, waits for them, and re-layouts  16.8 us (10%)
    pallas_call x1, Pallas kernels, reduced(): pl.pallas_call(reduce_kernel, out_shape=(jax.ShapeDtypeStruct((128, wide)...  69.3 us
    pallas_call x1, Pallas kernels, gathered_rows(): pl.pallas_call(gather_kernel, out_shape=(jax.ShapeDtypeStruct((rows, 2 *...  63.2 us
    unnamed x29, local copies, waits for them, and re-layouts  15.1 us
    pallas_call x1, Pallas kernels, heads_pass(): pl.pallas_call(heads_kernel, grid=(heads_here,), out_shape=(jax.ShapeDtyp...  12.1 us

profile of v3, /device:TPU:0, one launch (start us, length us, event | category | flops | bytes accessed | tf_op | source)
XLA Modules:
  0.0 162.1 jit_solution(3437018604954260996)
XLA Ops:
  0.6 0.7 broadcast_in_dim.13
  1.4 0.1 copy.11.flags_ref
  1.5 0.8 copy.12.seg_col_ref
  2.3 0.0 copy-start.5
  2.4 1.2 copy-done.5
  3.6 1.2 copy-done.6
  4.8 0.7 copy-done.10
  5.5 63.2 %shard_map.94 = (bf16[512,2048]{1,0:T(8,128)(2,1)S(1)}, bf16[512,2048]{1,0:T(8,128)(2,1)}, bf16[512,2048]{1,0:T(8,128)(2,1)}, f32[512,1536]{1,0:T(8,128)}, f32[512,1]{1,0:T(8,128)S(1)}, /*index=5*/f32[512,1]{1,0:T(8,128)S(1)}) custom-call(bf16[512,1024]{1,0:T(8,128)(2,1)S(1)} %copy-done.5, bf16[512,1024]{1,0:T(8,128)(2,1)S(1)} %copy-done.6, ...), custom_call_target="tpu_custom_call" | custom-call | tf_op jit(solution)/shard_map/pallas_call | solution.py:455
  68.7 0.0 copy-start.9
  68.7 0.7 copy-done.9
  69.4 0.0 copy-done.3
  69.4 0.0 copy-done.11
  69.4 0.0 copy-start
  69.4 2.4 %copy-done = bf16[512,2048]{1,0:T(8,128)(2,1)S(1)} copy-done((bf16[512,2048]{1,0:T(8,128)(2,1)S(1)}, bf16[512,2048]{1,0:T(8,128)(2,1)}, u32[]{:S(2)}) %copy-start) | copy-done | bytes 2097176
  71.8 1.9 %copy-done.1 = f32[512,1536]{1,0:T(8,128)S(1)} copy-done((f32[512,1536]{1,0:T(8,128)S(1)}, f32[512,1536]{1,0:T(8,128)}, u32[]{:S(2)}) %copy-start.1) | copy-done | bytes 3145752
  73.7 12.1 %shard_map.95 = (bf16[512,1536]{1,0:T(8,128)(2,1)S(1)}, bf16[512,512]{1,0:T(8,128)(2,1)S(1)}) custom-call(f32[512,1536]{1,0:T(8,128)S(1)} %copy-done.1, bf16[512,2048]{1,0:T(8,128)(2,1)S(1)} %copy-done, bf16[512,2048]{1,0:T(8,128)(2,1)S(1)} %copy-done.3, s32[512,1]{1,0:T(8,128)S(1)} %copy.12.seg_col_ref, s32[1,512]{1,0:T(1,128)S(1)} %bitcast.9), custom_call_target="tpu_custom_call" | custom-call | tf_op jit(solution)/shard_map/pallas_call | solution.py:524
  85.8 0.0 copy-done.2
  85.8 1.1 copy-done.4
  87.0 0.8 copy-done.7
  87.8 69.3 %shard_map.96 = (f32[128,1536]{1,0:T(8,128)}, f32[128,512]{1,0:T(8,128)}, bf16[512,1024]{1,0:T(8,128)(2,1)}) custom-call(bf16[512,2048]{1,0:T(8,128)(2,1)} %get-tuple-element.14.normed_ref, bf16[512,1536]{1,0:T(8,128)(2,1)} %copy-done.4, bf16[512,2048]{1,0:T(8,128)(2,1)} %get-tuple-element.16.dy_ref, bf16[512,512]{1,0:T(8,128)(2,1)} %copy-done.7, ...), custom_call_target="tpu_custom_call" | custom-call | tf_op jit(solution)/shard_map/pallas_call | solution.py:327
  157.0 0.0 copy-start.12
  157.1 1.9 %copy.13 = f32[512,128]{1,0:T(8,128)} copy(f32[512,128]{0,1:T(8,128)} %bitcast.10) | data formatting | bytes 524288
  158.9 2.3 %copy.16 = bf16[512,1024]{1,0:T(8,128)(2,1)} copy(bf16[512,1024]{1,0:T(8,128)(2,1)} %get-tuple-element.34) | data formatting | bytes 2097152
  161.2 0.9 copy.17
  (11 shorter events, 0.0 us)
Async XLA Ops:
  2.3 1.2 copy-start.5
  3.6 1.2 copy-start.6
  4.8 0.7 copy-start.10
  5.5 63.9 %copy-start.3 = (bf16[512,2048]{1,0:T(8,128)(2,1)S(1)}, bf16[512,2048]{1,0:T(8,128)(2,1)}, u32[]{:S(2)}) copy-start(bf16[512,2048]{1,0:T(8,128)(2,1)} %w_ref.4) | copy-start | bytes 6291460
  5.5 63.9 %copy-start.11 = (s32[512]{0:T(512)S(1)}, s32[512]{0:T(512)}, u32[]{:S(2)}) copy-start(s32[512]{0:T(512)} %param.10) | copy-start | bytes 6148
  68.7 0.7 copy-start.9
  69.4 16.4 %copy-start.2 = (bf16[512,2048]{1,0:T(8,128)(2,1)}, bf16[512,2048]{1,0:T(8,128)(2,1)S(1)}, u32[]{:S(2)}) copy-start(bf16[512,2048]{1,0:T(8,128)(2,1)S(1)} %get-tuple-element.19.x_ref) | copy-start | bytes 6291460
  69.4 16.4 %copy-start.8 = (f32[512,1]{1,0:T(8,128)}, f32[512,1]{1,0:T(8,128)S(1)}, u32[]{:S(2)}) copy-start(f32[512,1]{1,0:T(8,128)S(1)} %get-tuple-element.20.mean_ref) | copy-start | bytes 6148
  69.4 2.4 %copy-start = (bf16[512,2048]{1,0:T(8,128)(2,1)S(1)}, bf16[512,2048]{1,0:T(8,128)(2,1)}, u32[]{:S(2)}) copy-start(bf16[512,2048]{1,0:T(8,128)(2,1)} %get-tuple-element.16.dy_ref) | copy-start | bytes 6291460
  71.8 1.9 %copy-start.1 = (f32[512,1536]{1,0:T(8,128)S(1)}, f32[512,1536]{1,0:T(8,128)}, u32[]{:S(2)}) copy-start(f32[512,1536]{1,0:T(8,128)} %get-tuple-element.15.pre_ref) | copy-start | bytes 9437188
  85.8 1.1 copy-start.4
  87.0 0.8 copy-start.7
  157.0 4.1 %copy-start.12 = (f32[128,1536]{1,0:T(8,128)S(1)}, f32[128,1536]{1,0:T(8,128)}, u32[]{:S(2)}) copy-start(f32[128,1536]{1,0:T(8,128)} %get-tuple-element.35) | copy-start | bytes 2359300

commit v4 on v3

--- a/solution.py
+++ b/solution.py
@@ -466,7 +466,7 @@
         out_specs=[pl.BlockSpec(memory_space=pltpu.VMEM)] * 6,
         scratch_shapes=[landing] * 4 + [pltpu.SemaphoreType.DMA((4,))] * 6,
         compiler_params=pltpu.CompilerParams(
-            collective_id=1, has_side_effects=True, vmem_limit_bytes=48 * 1024 * 1024
+            collective_id=1, has_side_effects=True, vmem_limit_bytes=30 * 1024 * 1024
         ),
     )(inputs, grad_moved, flags, gain[None, :], proj_in)
 
@@ -539,7 +539,7 @@
             pl.BlockSpec((rows, span), lambda h: (0, h)),
             pl.BlockSpec((rows, DV), lambda h: (0, h)),
         ],
-        compiler_params=pltpu.CompilerParams(vmem_limit_bytes=40 * 1024 * 1024),
+        compiler_params=pltpu.CompilerParams(vmem_limit_bytes=26 * 1024 * 1024),
     )(pre, full_dy, proj_out, segments[:, None], segments[None, :])
 
 

time: 162 us -> 154 us (0.951)
  Pallas kernels: 145 us -> 139 us
  local copies, waits for them, and re-layouts: 16.8 us -> 14.6 us
    pallas_call x1, Pallas kernels: 63.2 us -> 57.3 us  [gathered_rows(): pl.pallas_call(gather_kernel, out_shape=(jax.ShapeDtypeStruct((rows, 2 *...]
    unnamed x29 -> x31, local copies, waits for them, and re-layouts: 15.1 us -> 12.9 us
where the time goes in v4:
time: 154 us
  Pallas kernels  139 us (90%)
  local copies, waits for them, and re-layouts  14.6 us (9%)
    pallas_call x1, Pallas kernels, reduced(): pl.pallas_call(reduce_kernel, out_shape=(jax.ShapeDtypeStruct((128, wide)...  69.3 us
    pallas_call x1, Pallas kernels, gathered_rows(): pl.pallas_call(gather_kernel, out_shape=(jax.ShapeDtypeStruct((rows, 2 *...  57.3 us
    unnamed x31, local copies, waits for them, and re-layouts  12.9 us
    pallas_call x1, Pallas kernels, heads_pass(): pl.pallas_call(heads_kernel, grid=(heads_here,), out_shape=(jax.ShapeDtyp...  12.1 us

profile of v4, /device:TPU:0, one launch (start us, length us, event | category | flops | bytes accessed | tf_op | source)
XLA Modules:
  0.0 154.0 jit_solution(11887012540674236452)
XLA Ops:
  0.6 0.7 broadcast_in_dim.13
  1.4 0.1 copy.11.flags_ref
  1.5 0.8 copy.12.seg_col_ref
  2.3 0.0 copy-start
  2.4 2.8 %copy-done = bf16[2048,1536]{1,0:T(8,128)(2,1)S(1)} copy-done((bf16[2048,1536]{1,0:T(8,128)(2,1)S(1)}, bf16[2048,1536]{1,0:T(8,128)(2,1)}, u32[]{:S(2)}) %copy-start) | copy-done | bytes 6291480
  5.1 1.2 copy-done.6
  6.4 1.2 copy-done.7
  7.6 0.7 copy-done.11
  8.3 57.3 %shard_map.94 = (bf16[512,2048]{1,0:T(8,128)(2,1)S(1)}, bf16[512,2048]{1,0:T(8,128)(2,1)S(1)}, bf16[512,2048]{1,0:T(8,128)(2,1)S(1)}, f32[512,1536]{1,0:T(8,128)...) custom-call(bf16[512,1024]{1,0:T(8,128)(2,1)S(1)} %copy-done.6, bf16[512,1024]{1,0:T(8,128)(2,1)S(1)} %copy-done.7, ...), custom_call_target="tpu_custom_call" | custom-call | tf_op jit(solution)/shard_map/pallas_call | solution.py:455
  65.5 0.0 copy-start.1
  65.6 0.0 copy-start.2
  65.6 0.0 copy-start.3
  65.6 0.0 copy-start.9
  65.6 0.0 copy-start.10
  65.6 0.0 copy-done.4
  65.6 0.0 copy-done.12
  65.6 12.1 %shard_map.95 = (bf16[512,1536]{1,0:T(8,128)(2,1)S(1)}, bf16[512,512]{1,0:T(8,128)(2,1)S(1)}) custom-call(f32[512,1536]{1,0:T(8,128)S(1)} %get-tuple-element.15.pre_ref, bf16[512,2048]{1,0:T(8,128)(2,1)S(1)} %get-tuple-element.16.dy_ref, bf16[512,2048]{1,0:T(8,128)(2,1)S(1)} %copy-done.4, s32[512,1]{1,0:T(8,128)S(1)} %copy.12.seg_col_ref, s32[1,512]{1,0:T(1,128)S(1)} %bitcast.9), custom_call_target="tpu_custom_call" | custom-call | tf_op jit(solution)/shard_map/pallas_call | solution.py:524
  77.7 0.0 copy-done.1
  77.8 1.1 copy-done.5
  78.9 0.8 copy-done.8
  79.7 69.3 %shard_map.96 = (f32[128,1536]{1,0:T(8,128)}, f32[128,512]{1,0:T(8,128)}, bf16[512,1024]{1,0:T(8,128)(2,1)}) custom-call(bf16[512,2048]{1,0:T(8,128)(2,1)} %copy-done.3, bf16[512,1536]{1,0:T(8,128)(2,1)} %copy-done.5, bf16[512,2048]{1,0:T(8,128)(2,1)} %copy-done.1, bf16[512,512]{1,0:T(8,128)(2,1)} %copy-done.8, bf16[2048,1536]{1,0:T(8,128)(2,1)} %w_ref.5, ...), custom_call_target="tpu_custom_call" | custom-call | tf_op jit(solution)/shard_map/pallas_call | solution.py:327
  149.0 1.9 %copy.13 = f32[512,128]{1,0:T(8,128)} copy(f32[512,128]{0,1:T(8,128)} %bitcast.10) | data formatting | bytes 524288
  150.9 2.3 %copy.16 = bf16[512,1024]{1,0:T(8,128)(2,1)} copy(bf16[512,1024]{1,0:T(8,128)(2,1)} %get-tuple-element.34) | data formatting | bytes 2097152
  153.1 0.9 copy.17
  (13 shorter events, 0.0 us)
Async XLA Ops:
  2.3 2.8 %copy-start = (bf16[2048,1536]{1,0:T(8,128)(2,1)S(1)}, bf16[2048,1536]{1,0:T(8,128)(2,1)}, u32[]{:S(2)}) copy-start(bf16[2048,1536]{1,0:T(8,128)(2,1)} %w_ref.5) | copy-start | bytes 18874372
  5.1 1.2 copy-start.6
  6.4 1.2 copy-start.7
  7.6 0.7 copy-start.11
  8.3 57.3 %copy-start.4 = (bf16[512,2048]{1,0:T(8,128)(2,1)S(1)}, bf16[512,2048]{1,0:T(8,128)(2,1)}, u32[]{:S(2)}) copy-start(bf16[512,2048]{1,0:T(8,128)(2,1)} %w_ref.4) | copy-start | bytes 6291460
  8.3 57.3 %copy-start.12 = (s32[512]{0:T(512)S(1)}, s32[512]{0:T(512)}, u32[]{:S(2)}) copy-start(s32[512]{0:T(512)} %param.10) | copy-start | bytes 6148
  65.5 12.2 %copy-start.1 = (bf16[512,2048]{1,0:T(8,128)(2,1)}, bf16[512,2048]{1,0:T(8,128)(2,1)S(1)}, u32[]{:S(2)}) copy-start(bf16[512,2048]{1,0:T(8,128)(2,1)S(1)} %get-tuple-element.16.dy_ref) | copy-start | bytes 6291460
  65.6 12.2 %copy-start.2 = (bf16[512,2048]{1,0:T(8,128)(2,1)}, bf16[512,2048]{1,0:T(8,128)(2,1)S(1)}, u32[]{:S(2)}) copy-start(bf16[512,2048]{1,0:T(8,128)(2,1)S(1)} %get-tuple-element.19.x_ref) | copy-start | bytes 6291460
  65.6 12.2 %copy-start.3 = (bf16[512,2048]{1,0:T(8,128)(2,1)}, bf16[512,2048]{1,0:T(8,128)(2,1)S(1)}, u32[]{:S(2)}) copy-start(bf16[512,2048]{1,0:T(8,128)(2,1)S(1)} %get-tuple-element.14.normed_ref) | copy-start | bytes 6291460
  65.6 12.2 %copy-start.9 = (f32[512,1]{1,0:T(8,128)}, f32[512,1]{1,0:T(8,128)S(1)}, u32[]{:S(2)}) copy-start(f32[512,1]{1,0:T(8,128)S(1)} %get-tuple-element.20.mean_ref) | copy-start | bytes 6148
  65.6 12.2 %copy-start.10 = (f32[512,1]{1,0:T(8,128)}, f32[512,1]{1,0:T(8,128)S(1)}, u32[]{:S(2)}) copy-start(f32[512,1]{1,0:T(8,128)S(1)} %get-tuple-element.21.inv_ref) | copy-start | bytes 6148
  77.8 1.1 copy-start.5
  78.9 0.8 copy-start.8
  149.0 4.1 %copy-start.13 = (f32[128,1536]{1,0:T(8,128)S(1)}, f32[128,1536]{1,0:T(8,128)}, u32[]{:S(2)}) copy-start(f32[128,1536]{1,0:T(8,128)} %get-tuple-element.35) | copy-start | bytes 2359300
